TPU v7x, 512 devices: a whole 4x4x16 slice. The times are simulated.
512 devices in a mesh: rad: 32 (over z, core), ord: 16 (over y, x).
Axes of the slice: x: 4, y: 4, z: 16, core: 2. Of those that a mesh axis runs over, the one named last changes fastest.
Arguments:
- coefficients: bfloat16 [4, 256, 256, 2, 256], P(None, 'rad', 'ord'), may hold values from -0.05859375 to 0.05859375
- order_of_slot: int32 [256], replicated, may hold values from 0 to 255, as said below
Outputs:
- grid: bfloat16 [4, 2, 256, 384, 768], P(None, None, 'rad', 'ord')
Inputs may be any that keep to these rules, and one draw needn't show every extreme that they name: `order_of_slot`: each order 0 to 255 stands in exactly one slot; slots 2i and 2i+1 hold two orders that sum to 255.
All inputs are finite; a program needn't handle non-finite values.
Results may differ from a plain program's by a relative error of at most 0.0016.
Values may be sent and summed in bfloat16 or wider, within the bound.
A program may use at most 128 MiB of HBM per device.

v0:
```python
import math

import jax
import jax.numpy as jnp
from jax import lax
from jax.sharding import PartitionSpec as P

NLAT = 384
NLON = 768


HIGHEST = lax.Precision.HIGHEST


def padded(cells, sides, width):
    for axis, dim in sides:
        count = lax.axis_size(axis)
        ends = count - 1
        head = lax.slice_in_dim(cells, 0, width, axis=dim)
        tail = lax.slice_in_dim(cells, cells.shape[dim] - width, cells.shape[dim], axis=dim)
        cells = jnp.concatenate(
            [
                lax.ppermute(tail, axis, [(i, (i + 1) % count) for i in range(ends)]),
                cells,
                lax.ppermute(head, axis, [((i + 1) % count, i) for i in range(ends)]),
            ],
            axis=dim,
        )
    return cells


def legendre_table(orders, colatitude, degrees):
    cosines = jnp.cos(colatitude)
    sine_theta = jnp.sin(colatitude)
    order_float = orders.astype(jnp.float32)[:, None]
    factor_index = jnp.arange(1, degrees, dtype=jnp.int32)
    factor_float = factor_index.astype(jnp.float32)
    log_factors = jnp.log((2.0 * factor_float - 1.0) / (2.0 * factor_float))
    log_product = jnp.sum(
        jnp.where(factor_index[None, :] <= orders[:, None], log_factors[None, :], 0.0), axis=1
    )
    log_seed = (
        0.5 * jnp.log((2.0 * order_float + 1.0) / (4.0 * math.pi))
        + 0.5 * log_product[:, None]
        + order_float * jnp.log(sine_theta)[None, :]
    )
    order_square = order_float * order_float
    unit_seed = jnp.ones_like(log_seed)
    rescale_log = 10.0 * math.log(10.0)

    def advance(carry, degree):
        previous, earlier, log_scale = carry
        degree_float = degree.astype(jnp.float32)
        raising = jnp.sqrt(
            jnp.maximum(4.0 * degree_float * degree_float - 1.0, 1.0)
            / jnp.maximum(degree_float * degree_float - order_square, 1.0)
        )
        below = degree_float - 1.0
        lowering = jnp.sqrt(
            jnp.maximum(below * below - order_square, 0.0)
            / jnp.maximum(4.0 * below * below - 1.0, 1.0)
        )
        recurred = raising * (cosines[None, :] * previous - lowering * earlier)
        current = jnp.where(
            degree == orders[:, None], unit_seed, jnp.where(degree > orders[:, None], recurred, 0.0)
        )
        large_value = jnp.abs(current) > 10000000000.0
        factor = jnp.where(large_value, 1e-10, 1.0)
        current = current * factor
        previous = previous * factor
        log_scale = log_scale + jnp.where(large_value, rescale_log, 0.0)
        return ((current, previous, log_scale), current * jnp.exp(log_scale))

    blank = jnp.zeros_like(log_seed)
    _, stacked = lax.scan(
        advance, (blank, blank, log_seed), jnp.arange(degrees, dtype=jnp.int32), unroll=16
    )
    return stacked


def fourier_table(orders, longitudes):
    product = orders[:, None] * jnp.arange(longitudes, dtype=jnp.int32)[None, :] % longitudes
    angles = 2.0 * math.pi / longitudes * product.astype(jnp.float32)
    weights = jnp.where(orders == 0, 1.0, 2.0).astype(jnp.float32)[:, None]
    return jnp.stack([weights * jnp.cos(angles), -weights * jnp.sin(angles)])


def colatitudes(count, total):
    return math.pi * (jnp.arange(count, dtype=jnp.float32) + 0.5) / total


def radial_slope(window, levels, axis):

    def shifted(offset):
        return lax.slice_in_dim(window, offset, offset + levels, axis=axis)

    return (shifted(0) - 8.0 * shifted(1) + 8.0 * shifted(3) - shifted(4)) / 12.0


def extend_levels(coefficients):
    return padded(coefficients, (("rad", 1),), 2)


def slope_fields(extended, levels):
    window = extended.astype(jnp.float32)
    center = lax.slice_in_dim(window, 2, levels + 2, axis=1)
    return jnp.stack([center, radial_slope(window, levels, 1)], axis=1)


def transform(fields, orders, colatitude, form):
    degrees = fields.shape[-1]
    legendre = legendre_table(orders, colatitude, degrees)
    return jnp.einsum(form, fields, legendre, precision=HIGHEST)


def body(coefficients, order_of_slot):
    potentials = coefficients.shape[0]
    levels = coefficients.shape[1]
    slots = coefficients.shape[2]
    order_devices = lax.axis_size("ord")
    lat_local = NLAT // order_devices
    all_slots = slots * order_devices
    own_orders = lax.dynamic_slice_in_dim(order_of_slot, lax.axis_index("ord") * slots, slots)
    waves = fourier_table(order_of_slot, NLON)
    every_lat = colatitudes(NLAT, NLAT)
    row_width = 2 * potentials * 2 * levels
    fields = slope_fields(extend_levels(coefficients), levels)
    spectral = transform(fields, own_orders, every_lat, "pqrmcl,lmj->mjcpqr")
    flat_values = spectral.reshape(slots, NLAT * row_width)
    arrived = lax.all_to_all(flat_values, "ord", split_axis=1, concat_axis=0, tiled=True)
    shaped = arrived.reshape(all_slots, lat_local, 2, potentials, 2, levels)
    gridded = jnp.einsum("mjcpqr,cmk->pqrjk", shaped, waves, precision=HIGHEST)
    return gridded.astype(jnp.bfloat16)


def solution(mesh):
    return jax.shard_map(
        body,
        mesh=mesh,
        in_specs=(P(None, "rad", "ord", None, None), P()),
        out_specs=P(None, None, "rad", "ord", None),
        check_vma=False,
    )
```

profile of v0, /device:TPU:6, one launch (start us, length us, event | category | flops | bytes accessed | tf_op | source)
XLA Modules:
  0.0 530.7 jit_solution(2168850894970670566)
XLA Ops:
  0.0 1.6 copy.25
  1.8 1.7 collective-permute-start
  3.5 1.3 collective-permute-start.1
  6.0 379.2 %while.21 = (s32[]{:T(128)}, f32[16,384]{1,0:T(8,128)S(1)}, f32[16,384]{1,0:T(8,128)S(1)}, f32[16,384]{1,0:T(8,128)S(1)}, f32[16,16,16,384]{3,2,1,0:T(8,128)}, /...) while((s32[]{:T(128)}, f32[16,384]{1,0:T(8,128)S(1)}, ...), condition=%wide.region_2.3_spmd.clone.clone, body=%wide.region_1.2_spmd.clone.clone.sunk | while | flops 3591106 | bytes 3061102 | solution.py:75
  13.2 10.0 %broadcast_compare_fusion.33 = (pred[16]{0:T(512)(128)(4,1)S(1)}, pred[16]{0:T(512)(128)(4,1)S(1)}, pred[16]{0:T(512)(128)(4,1)S(1)}, pred[16]{0:T(512)(128)(4,1...) fusion(s32[16]{0:T(128)S(1)} %get-tuple-element.733, ...), kind=kLoop, calls=%fused_computation.227.clone.1 | loop fusion | flops 512 | bytes 640 | tf_op jit(solution)/shard_map/while/body/eval_jaxpr/eq | solution.py:65
  36.9 10.0 %broadcast_compare_fusion.33 = (pred[16]{0:T(512)(128)(4,1)S(1)}, pred[16]{0:T(512)(128)(4,1)S(1)}, pred[16]{0:T(512)(128)(4,1)S(1)}, pred[16]{0:T(512)(128)(4,1...) fusion(s32[16]{0:T(128)S(1)} %get-tuple-element.733, ...), kind=kLoop, calls=%fused_computation.227.clone.1 | loop fusion | flops 512 | bytes 640 | tf_op jit(solution)/shard_map/while/body/eval_jaxpr/eq | solution.py:65
  60.5 10.0 %broadcast_compare_fusion.33 = (pred[16]{0:T(512)(128)(4,1)S(1)}, pred[16]{0:T(512)(128)(4,1)S(1)}, pred[16]{0:T(512)(128)(4,1)S(1)}, pred[16]{0:T(512)(128)(4,1...) fusion(s32[16]{0:T(128)S(1)} %get-tuple-element.733, ...), kind=kLoop, calls=%fused_computation.227.clone.1 | loop fusion | flops 512 | bytes 640 | tf_op jit(solution)/shard_map/while/body/eval_jaxpr/eq | solution.py:65
  84.2 10.0 %broadcast_compare_fusion.33 = (pred[16]{0:T(512)(128)(4,1)S(1)}, pred[16]{0:T(512)(128)(4,1)S(1)}, pred[16]{0:T(512)(128)(4,1)S(1)}, pred[16]{0:T(512)(128)(4,1...) fusion(s32[16]{0:T(128)S(1)} %get-tuple-element.733, ...), kind=kLoop, calls=%fused_computation.227.clone.1 | loop fusion | flops 512 | bytes 640 | tf_op jit(solution)/shard_map/while/body/eval_jaxpr/eq | solution.py:65
  107.9 10.0 %broadcast_compare_fusion.33 = (pred[16]{0:T(512)(128)(4,1)S(1)}, pred[16]{0:T(512)(128)(4,1)S(1)}, pred[16]{0:T(512)(128)(4,1)S(1)}, pred[16]{0:T(512)(128)(4,1...) fusion(s32[16]{0:T(128)S(1)} %get-tuple-element.733, ...), kind=kLoop, calls=%fused_computation.227.clone.1 | loop fusion | flops 512 | bytes 640 | tf_op jit(solution)/shard_map/while/body/eval_jaxpr/eq | solution.py:65
  123.7 0.8 bitcast_dynamic-update-slice_fusion.2
  131.7 10.0 %broadcast_compare_fusion.33 = (pred[16]{0:T(512)(128)(4,1)S(1)}, pred[16]{0:T(512)(128)(4,1)S(1)}, pred[16]{0:T(512)(128)(4,1)S(1)}, pred[16]{0:T(512)(128)(4,1...) fusion(s32[16]{0:T(128)S(1)} %get-tuple-element.733, ...), kind=kLoop, calls=%fused_computation.227.clone.1 | loop fusion | flops 512 | bytes 640 | tf_op jit(solution)/shard_map/while/body/eval_jaxpr/eq | solution.py:65
  155.4 10.0 %broadcast_compare_fusion.33 = (pred[16]{0:T(512)(128)(4,1)S(1)}, pred[16]{0:T(512)(128)(4,1)S(1)}, pred[16]{0:T(512)(128)(4,1)S(1)}, pred[16]{0:T(512)(128)(4,1...) fusion(s32[16]{0:T(128)S(1)} %get-tuple-element.733, ...), kind=kLoop, calls=%fused_computation.227.clone.1 | loop fusion | flops 512 | bytes 640 | tf_op jit(solution)/shard_map/while/body/eval_jaxpr/eq | solution.py:65
  171.1 0.8 bitcast_dynamic-update-slice_fusion.2
  179.1 10.0 %broadcast_compare_fusion.33 = (pred[16]{0:T(512)(128)(4,1)S(1)}, pred[16]{0:T(512)(128)(4,1)S(1)}, pred[16]{0:T(512)(128)(4,1)S(1)}, pred[16]{0:T(512)(128)(4,1...) fusion(s32[16]{0:T(128)S(1)} %get-tuple-element.733, ...), kind=kLoop, calls=%fused_computation.227.clone.1 | loop fusion | flops 512 | bytes 640 | tf_op jit(solution)/shard_map/while/body/eval_jaxpr/eq | solution.py:65
  202.8 10.0 %broadcast_compare_fusion.33 = (pred[16]{0:T(512)(128)(4,1)S(1)}, pred[16]{0:T(512)(128)(4,1)S(1)}, pred[16]{0:T(512)(128)(4,1)S(1)}, pred[16]{0:T(512)(128)(4,1...) fusion(s32[16]{0:T(128)S(1)} %get-tuple-element.733, ...), kind=kLoop, calls=%fused_computation.227.clone.1 | loop fusion | flops 512 | bytes 640 | tf_op jit(solution)/shard_map/while/body/eval_jaxpr/eq | solution.py:65
  226.4 10.0 %broadcast_compare_fusion.33 = (pred[16]{0:T(512)(128)(4,1)S(1)}, pred[16]{0:T(512)(128)(4,1)S(1)}, pred[16]{0:T(512)(128)(4,1)S(1)}, pred[16]{0:T(512)(128)(4,1...) fusion(s32[16]{0:T(128)S(1)} %get-tuple-element.733, ...), kind=kLoop, calls=%fused_computation.227.clone.1 | loop fusion | flops 512 | bytes 640 | tf_op jit(solution)/shard_map/while/body/eval_jaxpr/eq | solution.py:65
  250.2 10.0 %broadcast_compare_fusion.33 = (pred[16]{0:T(512)(128)(4,1)S(1)}, pred[16]{0:T(512)(128)(4,1)S(1)}, pred[16]{0:T(512)(128)(4,1)S(1)}, pred[16]{0:T(512)(128)(4,1...) fusion(s32[16]{0:T(128)S(1)} %get-tuple-element.733, ...), kind=kLoop, calls=%fused_computation.227.clone.1 | loop fusion | flops 512 | bytes 640 | tf_op jit(solution)/shard_map/while/body/eval_jaxpr/eq | solution.py:65
  273.9 10.0 %broadcast_compare_fusion.33 = (pred[16]{0:T(512)(128)(4,1)S(1)}, pred[16]{0:T(512)(128)(4,1)S(1)}, pred[16]{0:T(512)(128)(4,1)S(1)}, pred[16]{0:T(512)(128)(4,1...) fusion(s32[16]{0:T(128)S(1)} %get-tuple-element.733, ...), kind=kLoop, calls=%fused_computation.227.clone.1 | loop fusion | flops 512 | bytes 640 | tf_op jit(solution)/shard_map/while/body/eval_jaxpr/eq | solution.py:65
  297.6 10.0 %broadcast_compare_fusion.33 = (pred[16]{0:T(512)(128)(4,1)S(1)}, pred[16]{0:T(512)(128)(4,1)S(1)}, pred[16]{0:T(512)(128)(4,1)S(1)}, pred[16]{0:T(512)(128)(4,1...) fusion(s32[16]{0:T(128)S(1)} %get-tuple-element.733, ...), kind=kLoop, calls=%fused_computation.227.clone.1 | loop fusion | flops 512 | bytes 640 | tf_op jit(solution)/shard_map/while/body/eval_jaxpr/eq | solution.py:65
  321.3 10.0 %broadcast_compare_fusion.33 = (pred[16]{0:T(512)(128)(4,1)S(1)}, pred[16]{0:T(512)(128)(4,1)S(1)}, pred[16]{0:T(512)(128)(4,1)S(1)}, pred[16]{0:T(512)(128)(4,1...) fusion(s32[16]{0:T(128)S(1)} %get-tuple-element.733, ...), kind=kLoop, calls=%fused_computation.227.clone.1 | loop fusion | flops 512 | bytes 640 | tf_op jit(solution)/shard_map/while/body/eval_jaxpr/eq | solution.py:65
  345.0 10.0 %broadcast_compare_fusion.33 = (pred[16]{0:T(512)(128)(4,1)S(1)}, pred[16]{0:T(512)(128)(4,1)S(1)}, pred[16]{0:T(512)(128)(4,1)S(1)}, pred[16]{0:T(512)(128)(4,1...) fusion(s32[16]{0:T(128)S(1)} %get-tuple-element.733, ...), kind=kLoop, calls=%fused_computation.227.clone.1 | loop fusion | flops 512 | bytes 640 | tf_op jit(solution)/shard_map/while/body/eval_jaxpr/eq | solution.py:65
  368.6 10.0 %broadcast_compare_fusion.33 = (pred[16]{0:T(512)(128)(4,1)S(1)}, pred[16]{0:T(512)(128)(4,1)S(1)}, pred[16]{0:T(512)(128)(4,1)S(1)}, pred[16]{0:T(512)(128)(4,1...) fusion(s32[16]{0:T(128)S(1)} %get-tuple-element.733, ...), kind=kLoop, calls=%fused_computation.227.clone.1 | loop fusion | flops 512 | bytes 640 | tf_op jit(solution)/shard_map/while/body/eval_jaxpr/eq | solution.py:65
  386.2 2.3 copy-done.1
  388.5 6.3 %fusion.91 = f32[16,384,2,4,2,8]{1,5,2,4,3,0:T(8,128)S(1)} fusion(f32[4,1,8,16,2,256]{5,2,4,1,0,3:T(8,128)S(1)} %get-tuple-element.427, f32[4,1,8,16,2,256]{5,2,4,1,0,3:T(8,128)S(1)} %get-tuple-element.426, f32[256,16,384,1,1,1]{2,1,0,5,4,3:T(8,128)S(1)} %bitcast.219), kind=kOutput, calls=%fused_computation.237 | convolution fusion | flops 2416443392 | bytes 11534336 | tf_op jit(solution)/shard_map/pqrmcl,lmj->mjcpqr/dot_general | solution.py:113
  394.9 19.7 %copy.30 = f32[16,384,2,4,2,8]{0,5,4,3,2,1:T(8,128)} copy(f32[16,384,2,4,2,8]{1,5,2,4,3,0:T(8,128)S(1)} %fusion.91) | data formatting | bytes 6291456 | tf_op jit(solution)/shard_map/pqrmcl,lmj->mjcpqr/transpose | solution.py:113
  414.6 14.9 %copy.31 = f32[16,16,3072]{2,0,1:T(8,128)} copy(f32[16,16,3072]{0,2,1:T(8,128)} %bitcast.217) | data formatting | bytes 6291456 | tf_op jit(solution)/shard_map/all_to_all | solution.py:130
  429.4 9.0 %all-to-all-start = ((f32[16,16,3072]{2,0,1:T(8,128)}), f32[16,16,3072]{2,0,1:T(8,128)S(1)}, u32[]{:S(2)}, u32[]{:S(2)}) async-start(f32[16,16,3072]{2,0,1:T(8,128)} %copy.31), calls=%async_computation | async-start | bytes 6291456 | tf_op jit(solution)/shard_map/all_to_all | solution.py:130
  438.5 4.4 cosine_multiply_fusion
  442.9 43.8 %all-to-all-done = f32[16,16,3072]{2,0,1:T(8,128)S(1)} async-done(((f32[16,16,3072]{2,0,1:T(8,128)}), f32[16,16,3072]{2,0,1:T(8,128)S(1)}, u32[]{:S(2)}, u32[]{:S(2)}) %all-to-all-start) | async-done | bytes 3145760 | tf_op jit(solution)/shard_map/all_to_all | solution.py:130
  486.7 12.5 %copy.32 = f32[16,16,3072]{1,0,2:T(8,128)} copy(f32[16,16,3072]{2,1,0:T(8,128)S(1)} %bitcast.218) | data formatting | bytes 6291456 | tf_op jit(solution)/shard_map/all_to_all | solution.py:130
  499.2 16.7 %reshape.1006 = f32[256,24,2,4,2,8]{0,5,4,3,2,1:T(8,128)S(1)} reshape(f32[16,16,3072]{1,0,2:T(8,128)} %copy.32) | data formatting | bytes 6291456 | tf_op jit(solution)/shard_map/reshape | solution.py:131
  515.9 14.9 %fusion.85 = bf16[4,2,8,24,768]{4,3,2,1,0:T(8,128)(2,1)} fusion(f32[256,24,2,4,2,8]{0,5,4,3,2,1:T(8,128)S(1)} %reshape.1006, f32[1,256,768]{2,1,0:T(8,128)} %get-tuple-element.431, f32[1,256,768]{2,1,0:T(8,128)} %get-tuple-element.430), kind=kOutput, calls=%fused_computation.233 | convolution fusion | flops 7249330176 | bytes 7077888 | tf_op jit(solution)/shard_map/mjcpqr,cmk->pqrjk/dot_general | solution.py:132
  (419 shorter events, 54.7 us)
Async XLA Ops:
  1.8 383.4 %collective-permute-start = (bf16[4,2,16,2,256]{4,1,3,0,2:T(2,128)(2,1)S(1)}, bf16[4,2,16,2,256]{4,1,3,0,2:T(2,128)(2,1)S(1)}, u32[]{:S(2)}, u32[]{:S(2)}) collective-permute-start(bf16[4,2,16,2,256]{4,1,3,0,2:T(2,128)(2,1)S(1)} %get-tuple-element.428), channel_id=1, source_target_pairs={{0,16},{16,32},{32,48},{48,64},{64,80},{80,96},{96,112},{112,128},... | collective-permute-start | bytes 393224 | tf_op jit(solution)/shard_map/ppermute | solution.py:23
  3.5 381.6 %collective-permute-start.1 = (bf16[4,2,16,2,256]{4,1,3,0,2:T(2,128)(2,1)S(1)}, bf16[4,2,16,2,256]{4,1,3,0,2:T(2,128)(2,1)S(1)}, u32[]{:S(2)}, u32[]{:S(2)}) collective-permute-start(bf16[4,2,16,2,256]{4,1,3,0,2:T(2,128)(2,1)S(1)} %get-tuple-element.429), channel_id=1, source_target_pairs={{16,0},{32,16},{48,32},{64,48},{80,64},{96,80},{112,96},{128,112},... | collective-permute-start | bytes 393224 | tf_op jit(solution)/shard_map/ppermute | solution.py:25
  385.7 2.8 copy-start.1
  429.4 9.1 %copy-start = (s32[256]{0:T(256)S(1)}, s32[256]{0:T(256)}, u32[]{:S(2)}) copy-start(s32[256]{0:T(256)} %param.5) | copy-start | bytes 3076
  429.4 57.3 %all-to-all-start = ((f32[16,16,3072]{2,0,1:T(8,128)}), f32[16,16,3072]{2,0,1:T(8,128)S(1)}, u32[]{:S(2)}, u32[]{:S(2)}) async-start(f32[16,16,3072]{2,0,1:T(8,128)} %copy.31), calls=%async_computation | async-start | bytes 6291456 | tf_op jit(solution)/shard_map/all_to_all | solution.py:130
where the time goes:
time: 539 us; the launch traced here: 531 us
  other arithmetic  196 us (36%)
  loops' own time  166 us (31%)
  local copies, waits for them, and re-layouts  92 us (17%)
  waiting for transfers between devices  43.8 us (8%)
  matrix products  21.2 us (4%)
  starting transfers between devices  12.1 us (2%)
    another operation x1, loops' own time, legendre_table(): lax.scan(advance, (blank, blank, log_seed), jnp.arange(degrees, dtype=jnp...  166 us
    eq x16, other arithmetic, advance(): degree == orders[:, None]  160 us
    all_to_all x1, waiting for transfers between devices, body(): lax.all_to_all(flat_values, 'ord', split_axis=1, concat_axis=0, tiled=True)  43.8 us
    all_to_all x2, local copies, waits for them, and re-layouts, body(): lax.all_to_all(flat_values, 'ord', split_axis=1, concat_axis=0, tiled=True)  27.4 us
    while x240, other arithmetic  25.3 us
    transpose x1, local copies, waits for them, and re-layouts, transform(): return jnp.einsum(form, fields, legendre, precision=HIGHEST)  19.7 us
    reshape x1, local copies, waits for them, and re-layouts, body(): shaped = arrived.reshape(all_slots, lat_local, 2, potentials, 2, levels)  16.7 us
    dot_general x1, matrix products, body(): gridded = jnp.einsum('mjcpqr,cmk->pqrjk', shaped, waves, precision=HIGHEST)  14.9 us
  transfers between devices with their start and end apart: 3, of which 1 were waited for; matrix products, arithmetic and copies ran while one was open for 41% of the time, Pallas kernels for 0%

commit v1 on v0

v1 whole, which is shorter than its diff:
```python
import math

import jax
import jax.numpy as jnp
from jax import lax
from jax.experimental import pallas as pl
from jax.experimental.pallas import tpu as pltpu
from jax.sharding import PartitionSpec as P

LDEG = 256
NLAT = 384
NLON = 768
HALF = NLON // 2
POT = 4
LEV = 8
SLOTS = 16
PAIRS = 8
ORD = 16
LAT = NLAT // ORD
PITCH = LDEG + 8
ROWS = PAIRS + PAIRS // 2 + 1
LN2 = math.log(2.0)
F32 = jnp.float32
BF16 = jnp.bfloat16


def split(x):
    high = x.astype(BF16)
    return high, (x - high.astype(F32)).astype(BF16)


def legendre_kernel(order_ref, own_ref, halo_ref, out_ref, table, sums):
    first = lax.axis_index("ord") * SLOTS
    slots, orders = [0] * SLOTS, [0] * SLOTS
    for g in range(PAIRS):
        head = order_ref[first + 2 * g]
        odd = head & 1
        even_order = jnp.where(odd == 0, head, LDEG - 1 - head)
        slots[g], slots[PAIRS + g] = 2 * g + odd, 2 * g + 1 - odd
        orders[g], orders[PAIRS + g] = even_order, LDEG - 1 - even_order
    row = lax.broadcasted_iota(jnp.int32, (SLOTS, 128), 0)
    order = jnp.zeros((SLOTS, 128), jnp.int32)
    for i in range(SLOTS):
        order = jnp.where(row == i, orders[i], order)
    m = jnp.concatenate([order, order], axis=1).astype(F32)
    degree = lax.broadcasted_iota(jnp.int32, (SLOTS, LDEG), 1).astype(F32)
    msq = m * m
    raising = jnp.sqrt(jnp.maximum(4.0 * degree * degree - 1.0, 1.0) / jnp.maximum(degree * degree - msq, 1.0))
    below = degree - 1.0
    lowering = jnp.sqrt(jnp.maximum(below * below - msq, 0.0) / jnp.maximum(4.0 * below * below - 1.0, 1.0))
    lowering = raising * lowering
    factor = jnp.maximum(degree, 1.0)
    logs = jnp.log((2.0 * factor - 1.0) / (2.0 * factor))
    logs = jnp.where((degree >= 1.0) & (degree <= m), logs, 0.0)
    product = jnp.sum(logs, axis=1, keepdims=True)
    lat = lax.broadcasted_iota(jnp.int32, (8, NLAT), 1).astype(F32)
    theta = math.pi * (lat + 0.5) / NLAT
    cosine = jnp.cos(theta)
    cosine = jnp.concatenate([cosine, cosine], axis=0)
    log_sine = jnp.log(jnp.sin(theta))
    log_sine = jnp.concatenate([log_sine, log_sine], axis=0)
    m1 = m[:, :1]
    scale = 0.5 * jnp.log((2.0 * m1 + 1.0) / (4.0 * math.pi)) + 0.5 * product + m1 * log_sine

    def block(step, carry):
        last, prior, scale = carry
        start = step * 8
        up = pltpu.roll(raising, LDEG - start, 1)
        down = pltpu.roll(lowering, LDEG - start, 1)
        growth = jnp.exp(scale)
        for j in range(8):
            seed = jnp.where(order == start + j, 1.0, 0.0)
            seed = jnp.concatenate([seed] * 3, axis=1)
            new = (up[:, j:j + 1] * cosine) * last + (seed - down[:, j:j + 1] * prior)
            value = new * growth
            for t in range(3):
                for h in range(2):
                    table[t, pl.ds(h * PAIRS * PITCH + start + j, 8, stride=PITCH), :] = value[8 * h:8 * h + 8, 128 * t:128 * t + 128]
            last, prior = new, last
        large = jnp.abs(last) > 1e10
        shrink = jnp.where(large, 1e-10, 1.0)
        return last * shrink, prior * shrink, scale + jnp.where(large, 10.0 * math.log(10.0), 0.0)

    blank = jnp.zeros((SLOTS, NLAT), F32)
    lax.fori_loop(0, LDEG // 8, block, (blank, blank, scale))

    top = jnp.zeros((8, NLAT), F32)
    for i in range(SLOTS):
        g, eo = i % PAIRS, i // PAIRS
        left = jnp.concatenate([own_ref[slots[i]], halo_ref[slots[i]]], axis=0)
        values = jnp.concatenate([table[t, pl.ds(i * PITCH, LDEG), :] for t in range(3)], axis=1)
        high, low = split(values)
        got = jnp.dot(left, high, preferred_element_type=F32) + jnp.dot(left, low, preferred_element_type=F32)
        top = jnp.maximum(top, jnp.max(jnp.abs(got.reshape(12, 8, NLAT)), axis=0))
        sums[g * 128 + 64 * eo:g * 128 + 64 * eo + 64, :] = got[:64]
        at = (PAIRS + g // 2) * 128 + 64 * (g % 2) + 32 * eo
        sums[at:at + 32, :] = got[64:]
    top = jnp.max(top, axis=0, keepdims=True)
    power = jnp.ceil(jnp.log(jnp.maximum(top, 1e-30)) * (1.0 / LN2) + 0.001) - 15.0
    inverse = jnp.exp(-LN2 * power) * 0.9999
    inverse = jnp.broadcast_to(inverse, (128, NLAT))
    power = jnp.broadcast_to(power, (128, NLAT))
    for k in range(ROWS):
        if k < ROWS - 1:
            coded = jnp.round(sums[k * 128:k * 128 + 128, :] * inverse)
        else:
            coded = power
        coded = jnp.concatenate([coded[:, 128 * t:128 * t + 128].T for t in range(3)], axis=0)
        coded = coded.astype(jnp.int32)
        for d in range(ORD):
            out_ref[d, k] = coded[d * LAT:d * LAT + LAT].astype(jnp.int16)


def fourier_kernel(coded_ref, high_ref, low_ref, out_ref, flat, halo_flat, own, halo):
    p = pl.program_id(0)

    @pl.when(p == 0)
    def _():
        for s in range(ORD):
            unit = jnp.exp(LN2 * coded_ref[s, ROWS - 1].astype(jnp.int32).astype(F32)) * (1.0 / 0.9999)
            for k in range(ROWS - 1):
                value = coded_ref[s, k].astype(jnp.int32).astype(F32) * unit
                if k < PAIRS:
                    at = (s * PAIRS + k) * LAT
                    flat[at:at + LAT, :] = value
                else:
                    at = (s * (PAIRS // 2) + k - PAIRS) * LAT
                    halo_flat[at:at + LAT, :] = value
        for i in range(LAT):
            even = flat[pl.ds(i, 64, stride=2 * LAT), :]
            odd = flat[pl.ds(LAT + i, 64, stride=2 * LAT), :]
            own[pl.ds(i, 128, stride=LAT), :] = jnp.concatenate([even, odd], axis=0).T
            edge = halo_flat[pl.ds(i, 64, stride=LAT), :]
            edge = jnp.concatenate([edge, pltpu.roll(edge, 64, 1)], axis=0).T
            halo[pl.ds(i, 64, stride=LAT), :] = edge[:64]

    def level(eo, c, r):
        if 0 <= r < LEV:
            at = (((eo * POT + p) * LEV + r) * 2 + c) * LAT
            return own[pl.ds(pl.multiple_of(at, 8), LAT), :]
        at = (((eo * POT + p) * 4 + (r + 2 if r < 0 else r - LEV + 2)) * 2 + c) * LAT
        return halo[pl.ds(pl.multiple_of(at, 8), LAT), :]

    totals = []
    for eo in range(2):
        parts = []
        for c in range(2):
            center = [level(eo, c, r) for r in range(-2, LEV + 2)]
            slope = [
                (center[r] - 8.0 * center[r + 1] + 8.0 * center[r + 3] - center[r + 4]) * (1.0 / 12.0)
                for r in range(LEV)
            ]
            parts.append(jnp.concatenate(center[2:-2] + slope, axis=0))
        high, low = split(jnp.concatenate(parts, axis=1))
        wave = high_ref[eo]
        total = jnp.dot(high, wave, preferred_element_type=F32)
        total += jnp.dot(low, wave, preferred_element_type=F32)
        total += jnp.dot(high, low_ref[eo], preferred_element_type=F32)
        totals.append(total)
    both = totals[0] + totals[1]
    out_ref[0, :, :, :, :HALF] = both.astype(BF16).reshape(2, LEV, LAT, HALF)
    both = totals[0] - totals[1]
    out_ref[0, :, :, :, HALF:] = both.astype(BF16).reshape(2, LEV, LAT, HALF)


def waves(order_of_slot):
    pair = order_of_slot.reshape(LDEG // 2, 2)
    even = jnp.where(pair[:, 0] % 2 == 0, pair[:, 0], pair[:, 1])
    even = even.reshape(LDEG // 4, 2).T.reshape(LDEG // 2)
    orders = jnp.stack([even, LDEG - 1 - even])
    product = orders[:, :, None] * jnp.arange(HALF, dtype=jnp.int32) % NLON
    angles = 2.0 * math.pi / NLON * product.astype(F32)
    weights = jnp.where(orders == 0, 1.0, 2.0).astype(F32)[:, :, None]
    table = jnp.concatenate([weights * jnp.cos(angles), -weights * jnp.sin(angles)], axis=1)
    high = lax.reduce_precision(table, 8, 7)
    return high.astype(BF16), (table - high).astype(BF16)


def body(coefficients, order_of_slot):
    count = lax.axis_size("rad")
    head = coefficients[:, :2]
    tail = coefficients[:, LEV - 2:]
    lower = lax.ppermute(tail, "rad", [(i, i + 1) for i in range(count - 1)])
    upper = lax.ppermute(head, "rad", [(i + 1, i) for i in range(count - 1)])
    own = jnp.transpose(coefficients, (2, 0, 1, 3, 4)).reshape(SLOTS, 64, LDEG)
    halo = jnp.concatenate([lower, upper], axis=1)
    halo = jnp.transpose(halo, (2, 0, 1, 3, 4)).reshape(SLOTS, 32, LDEG)
    vmem = pl.BlockSpec(memory_space=pltpu.VMEM)
    coded = pl.pallas_call(
        legendre_kernel,
        out_shape=jax.ShapeDtypeStruct((ORD, ROWS, LAT, 128), jnp.int16),
        in_specs=[pl.BlockSpec(memory_space=pltpu.SMEM), vmem, vmem],
        out_specs=vmem,
        scratch_shapes=[
            pltpu.VMEM((3, SLOTS * PITCH, 128), F32),
            pltpu.VMEM(((ROWS - 1) * 128, NLAT), F32),
        ],
    )(order_of_slot, own, halo)
    coded = lax.all_to_all(coded, "ord", split_axis=0, concat_axis=0, tiled=True)
    high, low = waves(order_of_slot)
    return pl.pallas_call(
        fourier_kernel,
        out_shape=jax.ShapeDtypeStruct((POT, 2, LEV, LAT, NLON), BF16),
        grid=(POT,),
        in_specs=[
            pl.BlockSpec((ORD, ROWS, LAT, 128), lambda p: (0, 0, 0, 0)),
            pl.BlockSpec((2, LDEG, HALF), lambda p: (0, 0, 0)),
            pl.BlockSpec((2, LDEG, HALF), lambda p: (0, 0, 0)),
        ],
        out_specs=pl.BlockSpec((1, 2, LEV, LAT, NLON), lambda p: (p, 0, 0, 0, 0)),
        scratch_shapes=[
            pltpu.VMEM((128 * LAT, 128), F32),
            pltpu.VMEM((64 * LAT, 128), F32),
            pltpu.VMEM((128 * LAT, 128), F32),
            pltpu.VMEM((64 * LAT, 128), F32),
        ],
    )(coded, high, low)


def solution(mesh):
    return jax.shard_map(
        body,
        mesh=mesh,
        in_specs=(P(None, "rad", "ord", None, None), P()),
        out_specs=P(None, None, "rad", "ord", None),
        check_vma=False,
    )
```

time: 539 us -> 61.9 us (0.11)
  the two profiles are of different devices: /device:TPU:6 before, /device:TPU:128 now
where the time goes in v1:
time: 61.9 us; the launch traced here: 61.6 us
  waiting for transfers between devices  20.1 us (32%)
  Pallas kernels  17.7 us (29%)
  starting transfers between devices  13.9 us (22%)
  local copies, waits for them, and re-layouts  6.49 us (10%)
  other arithmetic  3.14 us (5%)
    all_to_all x1, waiting for transfers between devices, body(): lax.all_to_all(coded, 'ord', split_axis=0, concat_axis=0, tiled=True)  20.1 us
    pallas_call x1, Pallas kernels, body(): pl.pallas_call(legendre_kernel, out_shape=jax.ShapeDtypeStruct((ORD, ROWS...  10.9 us
    all_to_all x1, starting transfers between devices, body(): lax.all_to_all(coded, 'ord', split_axis=0, concat_axis=0, tiled=True)  7.16 us
    pallas_call x1, Pallas kernels, body(): pl.pallas_call(fourier_kernel, out_shape=jax.ShapeDtypeStruct((POT, 2, LE...  6.81 us
    ppermute x1, starting transfers between devices, body(): upper = lax.ppermute(head, 'rad', [(i + 1, i) for i in range(count - 1)])  4.85 us
    ppermute x1, starting transfers between devices, body(): lower = lax.ppermute(tail, 'rad', [(i, i + 1) for i in range(count - 1)])  1.92 us
    mul x1, other arithmetic, waves(): weights * jnp.cos(angles)  1.71 us
    transpose x1, local copies, waits for them, and re-layouts, body(): own = jnp.transpose(coefficients, (2, 0, 1, 3, 4)).reshape(SLOTS, 64, LDEG)  1.52 us
  transfers between devices with their start and end apart: 3, of which 1 were waited for; matrix products, arithmetic and copies ran while one was open for 10% of the time, Pallas kernels for 0%

profile of v1, /device:TPU:128, one launch (start us, length us, event | category | flops | bytes accessed | tf_op | source)
XLA Modules:
  0.0 61.6 jit_solution(8343243528257566456)
XLA Ops:
  0.0 1.2 %fusion.10 = (bf16[4,2,16,2,256]{4,3,2,1,0:T(2,128)(2,1)S(1)}, bf16[4,2,16,2,256]{4,3,2,1,0:T(2,128)(2,1)S(1)}) fusion(bf16[4,8,16,2,256]{4,3,2,1,0:T(2,128)(2,1)} %param.2), kind=kLoop, calls=%fused_computation.27 | loop fusion | bytes 524288 | tf_op jit(solution)/shard_map/slice | solution.py:182
  1.2 1.9 %collective-permute-start = (bf16[4,2,16,2,256]{4,3,2,1,0:T(2,128)(2,1)S(1)}, bf16[4,2,16,2,256]{4,3,2,1,0:T(2,128)(2,1)S(1)}, u32[]{:S(2)}, u32[]{:S(2)}) collective-permute-start(bf16[4,2,16,2,256]{4,3,2,1,0:T(2,128)(2,1)S(1)} %get-tuple-element.9), channel_id=1, source_target_pairs={{0,16},{16,32},{32,48},{48,64},{64,80},{80,96},{96,112},{112,128},... | collective-permute-start | bytes 393224 | tf_op jit(solution)/shard_map/ppermute | solution.py:183
  3.1 4.9 %collective-permute-start.1 = (bf16[4,2,16,2,256]{4,3,2,1,0:T(2,128)(2,1)S(1)}, bf16[4,2,16,2,256]{4,3,2,1,0:T(2,128)(2,1)S(1)}, u32[]{:S(2)}, u32[]{:S(2)}) collective-permute-start(bf16[4,2,16,2,256]{4,3,2,1,0:T(2,128)(2,1)S(1)} %get-tuple-element.10), channel_id=1, source_target_pairs={{16,0},{32,16},{48,32},{64,48},{80,64},{96,80},{112,96},{128,112},... | collective-permute-start | bytes 393224 | tf_op jit(solution)/shard_map/ppermute | solution.py:184
  8.0 1.5 %copy.6 = bf16[16,4,8,2,256]{4,3,2,1,0:T(2,128)(2,1)S(1)} copy(bf16[16,4,8,2,256]{4,3,0,2,1:T(2,128)(2,1)} %bitcast.5) | data formatting | bytes 1048576 | tf_op jit(solution)/shard_map/transpose | solution.py:185
  9.5 1.0 %reshape.53.own_ref = bf16[16,64,256]{2,1,0:T(8,128)(2,1)} reshape(bf16[16,4,8,2,256]{4,3,2,1,0:T(2,128)(2,1)S(1)} %copy.6) | data formatting | bytes 1048576 | tf_op jit(solution)/shard_map/reshape | solution.py:185
  10.5 0.0 collective-permute-done
  10.5 0.0 collective-permute-done.1
  10.5 0.3 maximum_bitcast_fusion
  10.8 0.2 copy.7
  11.1 0.8 %reshape.54.halo_ref = bf16[16,32,256]{2,1,0:T(8,128)(2,1)} reshape(bf16[16,4,4,2,256]{4,3,2,1,0:T(2,128)(2,1)S(1)} %copy.7) | data formatting | bytes 524288 | tf_op jit(solution)/shard_map/reshape | solution.py:187
  11.9 10.9 %shard_map.28 = s16[16,13,24,128]{3,2,1,0:T(8,128)(2,1)} custom-call(s32[256]{0:T(256)} %order_ref.1, bf16[16,64,256]{2,1,0:T(8,128)(2,1)} %reshape.53.own_ref, bf16[16,32,256]{2,1,0:T(8,128)(2,1)} %reshape.54.halo_ref), custom_call_target="tpu_custom_call" | custom-call | tf_op jit(solution)/shard_map/pallas_call | solution.py:189
  22.8 0.0 copy-start.1
  22.8 7.2 %all-to-all-start = ((s16[16,13,24,128]{3,2,1,0:T(8,128)(2,1)}), s16[16,13,24,128]{3,2,1,0:T(8,128)(2,1)S(1)}, u32[]{:S(2)}, u32[]{:S(2)}) async-start(s16[16,13,24,128]{3,2,1,0:T(8,128)(2,1)} %shard_map.28), calls=%async_computation | async-start | bytes 2555904 | tf_op jit(solution)/shard_map/all_to_all | solution.py:199
  30.0 0.0 copy-done.1
  30.0 0.1 reshape.55
  30.1 0.2 slice_reduce_fusion
  30.3 0.1 squeeze.8
  30.5 0.1 squeeze.7
  30.6 0.1 copy.8
  30.7 0.1 stack.6
  30.8 1.7 %cosine_multiply_fusion = (f32[2,128,384]{2,1,0:T(8,128)S(1)}, f32[2,128,384]{2,1,0:T(8,128)S(1)}) fusion(s32[2,128]{1,0:T(2,128)S(1)} %pad_add_fusion, f32[2,128]{1,0:T(2,128)S(1)} %get-tuple-element.13, f32[2,128]{1,0:T(2,128)S(1)} %get-tuple-element.14), kind=kLoop, calls=%fused_computation.8 | loop fusion | flops 1081344 | bytes 789504 | tf_op jit(solution)/shard_map/mul | solution.py:174
  32.5 1.0 %fusion = (bf16[2,256,384]{2,1,0:T(8,128)(2,1)}, bf16[2,256,384]{2,1,0:T(8,128)(2,1)}) fusion(f32[2,128,384]{2,1,0:T(8,128)S(1)} %get-tuple-element.12, f32[2,128,384]{2,1,0:T(8,128)S(1)} %get-tuple-element.11), kind=kLoop, calls=%fused_computation.2 | loop fusion | flops 983040 | bytes 1572864 | tf_op jit(solution)/shard_map/convert_element_type | solution.py:176
  33.6 20.1 %all-to-all-done.coded_ref = s16[16,13,24,128]{3,2,1,0:T(8,128)(2,1)S(1)} async-done(((s16[16,13,24,128]{3,2,1,0:T(8,128)(2,1)}), s16[16,13,24,128]{3,2,1,0:T(8,128)(2,1)S(1)}, u32[]{:S(2)}, u32[]{:S(2)}) %all-to-all-start) | async-done | bytes 1277984 | tf_op jit(solution)/shard_map/all_to_all | solution.py:199
  53.7 0.0 copy-start
  53.7 1.0 %copy-done = s16[16,13,24,128]{3,2,1,0:T(8,128)(2,1)} copy-done((s16[16,13,24,128]{3,2,1,0:T(8,128)(2,1)}, s16[16,13,24,128]{3,2,1,0:T(8,128)(2,1)S(1)}, u32[]{:S(2)}) %copy-start) | copy-done | bytes 1277976
  54.8 6.8 %shard_map.29 = bf16[4,2,8,24,768]{4,3,2,1,0:T(8,128)(2,1)} custom-call(s16[16,13,24,128]{3,2,1,0:T(8,128)(2,1)} %copy-done, bf16[2,256,384]{2,1,0:T(8,128)(2,1)} %get-tuple-element.8.high_ref, bf16[2,256,384]{2,1,0:T(8,128)(2,1)} %get-tuple-element.7.low_ref), custom_call_target="tpu_custom_call" | custom-call | tf_op jit(solution)/shard_map/pallas_call | solution.py:201
  (4 shorter events, 0.1 us)
Async XLA Ops:
  1.2 9.3 %collective-permute-start = (bf16[4,2,16,2,256]{4,3,2,1,0:T(2,128)(2,1)S(1)}, bf16[4,2,16,2,256]{4,3,2,1,0:T(2,128)(2,1)S(1)}, u32[]{:S(2)}, u32[]{:S(2)}) collective-permute-start(bf16[4,2,16,2,256]{4,3,2,1,0:T(2,128)(2,1)S(1)} %get-tuple-element.9), channel_id=1, source_target_pairs={{0,16},{16,32},{32,48},{48,64},{64,80},{80,96},{96,112},{112,128},... | collective-permute-start | bytes 393224 | tf_op jit(solution)/shard_map/ppermute | solution.py:183
  3.1 7.4 %collective-permute-start.1 = (bf16[4,2,16,2,256]{4,3,2,1,0:T(2,128)(2,1)S(1)}, bf16[4,2,16,2,256]{4,3,2,1,0:T(2,128)(2,1)S(1)}, u32[]{:S(2)}, u32[]{:S(2)}) collective-permute-start(bf16[4,2,16,2,256]{4,3,2,1,0:T(2,128)(2,1)S(1)} %get-tuple-element.10), channel_id=1, source_target_pairs={{16,0},{32,16},{48,32},{64,48},{80,64},{96,80},{112,96},{128,112},... | collective-permute-start | bytes 393224 | tf_op jit(solution)/shard_map/ppermute | solution.py:184
  22.8 7.2 %copy-start.1 = (s32[256]{0:T(256)S(1)}, s32[256]{0:T(256)}, u32[]{:S(2)}) copy-start(s32[256]{0:T(256)} %order_ref.1) | copy-start | bytes 3076
  22.8 30.9 %all-to-all-start = ((s16[16,13,24,128]{3,2,1,0:T(8,128)(2,1)}), s16[16,13,24,128]{3,2,1,0:T(8,128)(2,1)S(1)}, u32[]{:S(2)}, u32[]{:S(2)}) async-start(s16[16,13,24,128]{3,2,1,0:T(8,128)(2,1)} %shard_map.28), calls=%async_computation | async-start | bytes 2555904 | tf_op jit(solution)/shard_map/all_to_all | solution.py:199
  53.7 1.0 %copy-start = (s16[16,13,24,128]{3,2,1,0:T(8,128)(2,1)}, s16[16,13,24,128]{3,2,1,0:T(8,128)(2,1)S(1)}, u32[]{:S(2)}) copy-start(s16[16,13,24,128]{3,2,1,0:T(8,128)(2,1)S(1)} %all-to-all-done.coded_ref) | copy-start | bytes 3833860

commit v2 on v1

v2 whole, which is shorter than its diff:
```python
import math

import jax
import jax.numpy as jnp
from jax import lax
from jax.experimental import pallas as pl
from jax.experimental.pallas import tpu as pltpu
from jax.sharding import PartitionSpec as P

LDEG = 256
NLAT = 384
NLON = 768
HALF = NLON // 2
POT = 4
LEV = 8
SLOTS = 16
PAIRS = 8
ORD = 16
SIDE = 4
LAT = NLAT // ORD
NORTH = NLAT // 2
ROWS = 9
SCALE_ROW = 2
EDGE = 3
LN2 = math.log(2.0)
F32 = jnp.float32
BF16 = jnp.bfloat16
MESH = pl.DeviceIdType.MESH


def split(x):
    high = x.astype(BF16)
    return high, (x - high.astype(F32)).astype(BF16)


def legendre_kernel(order_ref, own_ref, out_ref, table, sums):
    first = lax.axis_index("ord") * SLOTS
    slots, orders = [0] * SLOTS, [0] * SLOTS
    for g in range(PAIRS):
        head = order_ref[first + 2 * g]
        odd = head & 1
        even_order = jnp.where(odd == 0, head, LDEG - 1 - head)
        slots[g], slots[PAIRS + g] = 2 * g + odd, 2 * g + 1 - odd
        orders[g], orders[PAIRS + g] = even_order, LDEG - 1 - even_order
    row = lax.broadcasted_iota(jnp.int32, (SLOTS, 128), 0)
    order = jnp.zeros((SLOTS, 128), jnp.int32)
    for i in range(SLOTS):
        order = jnp.where(row == i, orders[i], order)
    m = jnp.concatenate([order, order], axis=1).astype(F32)
    degree = lax.broadcasted_iota(jnp.int32, (SLOTS, LDEG), 1).astype(F32)
    msq = m * m
    raising = jnp.sqrt(jnp.maximum(4.0 * degree * degree - 1.0, 1.0) / jnp.maximum(degree * degree - msq, 1.0))
    below = degree - 1.0
    lowering = jnp.sqrt(jnp.maximum(below * below - msq, 0.0) / jnp.maximum(4.0 * below * below - 1.0, 1.0))
    lowering = raising * lowering
    factor = jnp.maximum(degree, 1.0)
    logs = jnp.log((2.0 * factor - 1.0) / (2.0 * factor))
    logs = jnp.where((degree >= 1.0) & (degree <= m), logs, 0.0)
    product = jnp.sum(logs, axis=1, keepdims=True)
    base = 0.5 * jnp.log((2.0 * m[:, :128] + 1.0) / (4.0 * math.pi)) + 0.5 * product

    lane = lax.broadcasted_iota(jnp.int32, (8, 128), 1)
    half = lane < 64

    def tiles(x):
        return [x[:8, :128], x[8:, :128], jnp.where(half, x[:8, :128], x[8:, :128])]

    theta = [math.pi * (lane.astype(F32) + 0.5) / NLAT, math.pi * ((lane & 63).astype(F32) + 128.5) / NLAT]
    cosine = [jnp.cos(t) for t in theta]
    log_sine = [jnp.log(jnp.sin(t)) for t in theta]
    cosine = [cosine[0], cosine[0], cosine[1]]
    log_sine = [log_sine[0], log_sine[0], log_sine[1]]
    order_tiles = tiles(order)
    start_scale = [b + k * s for b, k, s in zip(tiles(base), tiles(m), log_sine)]

    def block(step, carry):
        last, prior, scale = [list(c) for c in carry]
        start = step * 8
        up = pltpu.roll(raising, LDEG - start, 1)
        down = pltpu.roll(lowering, LDEG - start, 1)
        growth = [jnp.exp(s) for s in scale]
        for j in range(8):
            at = pl.multiple_of((start + j) * 8, 8)
            ups = tiles(jnp.broadcast_to(up[:, j:j + 1], (SLOTS, 128)))
            downs = tiles(jnp.broadcast_to(down[:, j:j + 1], (SLOTS, 128)))
            for t in range(3):
                seed = jnp.where(order_tiles[t] == start + j, 1.0, 0.0)
                new = (ups[t] * cosine[t]) * last[t] + (seed - downs[t] * prior[t])
                table[t, pl.ds(at, 8), :] = new * growth[t]
                last[t], prior[t] = new, last[t]
        for t in range(3):
            large = jnp.abs(last[t]) > 1e10
            shrink = jnp.where(large, 1e-10, 1.0)
            last[t], prior[t] = last[t] * shrink, prior[t] * shrink
            scale[t] = scale[t] + jnp.where(large, 10.0 * math.log(10.0), 0.0)
        return tuple(last), tuple(prior), tuple(scale)

    blank = tuple(jnp.zeros((8, 128), F32) for _ in range(3))
    lax.fori_loop(0, LDEG // 8, block, (blank, blank, tuple(start_scale)))

    parity = lax.broadcasted_iota(jnp.int32, (64, LDEG), 1) & 1
    parity = parity.astype(F32).astype(BF16)
    wide = lax.broadcasted_iota(jnp.int32, (64, 128), 1) < 64
    top = [jnp.zeros((8, 128), F32) for _ in range(3)]
    for g in range(PAIRS):
        shared = table[2, pl.ds(g, LDEG, stride=8), :]
        for eo in range(2):
            left = own_ref[slots[eo * PAIRS + g]]
            odd_left = left * parity
            left = jnp.concatenate([left - odd_left, odd_left], axis=0)
            values = jnp.concatenate([table[eo, pl.ds(g, LDEG, stride=8), :], shared], axis=1)
            right = jnp.concatenate(split(values), axis=0)
            got = jnp.dot(jnp.concatenate([left, left], axis=1), right, preferred_element_type=F32)
            north = got[:64] + got[64:]
            south = got[:64] - got[64:] if eo == 0 else got[64:] - got[:64]
            near, far = north[:, 128:], south[:, 128:]
            if eo == 0:
                mixed = jnp.where(wide, near, pltpu.roll(far, 64, 1))
            else:
                mixed = jnp.where(wide, pltpu.roll(near, 64, 1), far)
            at = (2 * g + eo) * 64
            for t, part in enumerate((north[:, :128], south[:, :128], mixed)):
                sums[t, at:at + 64, :] = part
                top[t] = jnp.maximum(top[t], jnp.max(jnp.abs(part.reshape(8, 8, 128)), axis=0))

    for t in range(3):
        peak = jnp.max(top[t], axis=0, keepdims=True)
        power = jnp.ceil(jnp.log(jnp.maximum(peak, 1e-30)) * (1.0 / LN2) + 0.001) - 15.0
        inverse = jnp.broadcast_to(jnp.exp(-LN2 * power) * 0.9999, (128, 128))
        for k in range(ROWS):
            if k == SCALE_ROW:
                coded = jnp.broadcast_to(power, (128, 128))
            else:
                pieces = []
                if k < SCALE_ROW:
                    picks = [(2 * q + k, eo, r) for q in range(4) for eo in range(2) for r in (0, 1)]
                elif k < SCALE_ROW + EDGE:
                    picks = [(2 * q + k - EDGE, eo, r) for q in range(4) for eo in range(2) for r in (6, 7)]
                else:
                    picks = [(4 * h + k - 5, eo, r) for h in range(2) for eo in range(2) for r in (2, 3, 4, 5)]
                for g, eo, r in picks:
                    pieces.append(sums[t, pl.ds((2 * g + eo) * 64 + r, 8, stride=8), :])
                coded = jnp.round(jnp.concatenate(pieces, axis=0) * inverse)
            coded = coded.T.astype(jnp.int32)
            if t < 2:
                spans = [(d, 0, LAT, LAT * d) for d in range(5)] + [(5, 0, 8, 120)]
                spans = [(d if t == 0 else ORD - 1 - d, lo, hi, at) for d, lo, hi, at in spans]
            else:
                spans = [(5, 8, LAT, 0), (6, 0, LAT, 16), (7, 0, LAT, 40)]
                spans = spans + [(ORD - 1 - d, lo, hi, at + 64) for d, lo, hi, at in spans]
            for d, lo, hi, at in spans:
                out_ref[d, k, lo:hi, :] = coded[at:at + hi - lo].astype(jnp.int16)


def turn(product):
    rest = product - NLON * jnp.floor(product * (1.0 / NLON))
    quarter = jnp.floor(rest * (1.0 / 192.0) + 0.5)
    x = (rest - 192.0 * quarter) * (2.0 * math.pi / NLON)
    y = x * x
    sine = x * (1.0 + y * (-1.0 / 6.0 + y * (1.0 / 120.0 + y * (-1.0 / 5040.0 + y * (1.0 / 362880.0)))))
    cosine = 1.0 + y * (-0.5 + y * (1.0 / 24.0 + y * (-1.0 / 720.0 + y * (1.0 / 40320.0 - y * (1.0 / 3628800.0)))))
    swap = (quarter == 1.0) | (quarter == 3.0)
    first = jnp.where(swap, sine, cosine)
    second = jnp.where(swap, cosine, sine)
    first = jnp.where((quarter == 1.0) | (quarter == 2.0), -first, first)
    second = jnp.where((quarter == 2.0) | (quarter == 3.0), -second, second)
    return first, second


def wave_tables(order_ref, main_ref, tail_ref):
    row = lax.broadcasted_iota(jnp.int32, (128, LDEG), 0)
    lane = lax.broadcasted_iota(jnp.int32, (128, LDEG), 1)
    source = (row & 15) * SLOTS + 2 * (row >> 4)
    heads = jnp.broadcast_to(order_ref[...], (128, LDEG)).astype(F32)
    head = jnp.sum(jnp.where(lane == source, heads, 0.0), axis=1, keepdims=True)
    even = jnp.where(head - 2.0 * jnp.floor(0.5 * head) == 0.0, head, LDEG - 1 - head)
    for eo in range(2):
        order = jnp.broadcast_to(even if eo == 0 else LDEG - 1 - even, (128, 128))
        weight = jnp.where(order == 0.0, 1.0, 2.0)
        for j in range(3):
            k = lax.broadcasted_iota(jnp.int32, (128, 128), 1).astype(F32) + 128.0 * j
            cosine, sine = turn(order * k)
            for c, wave in enumerate((weight * cosine, -weight * sine)):
                high, low = split(wave)
                at = c * 128
                if j < 2:
                    columns = pl.ds(128 * j, 128)
                    main_ref[eo, at:at + 128, columns] = high
                    main_ref[eo, LDEG + at:LDEG + at + 128, columns] = high
                    main_ref[eo, 2 * LDEG + at:2 * LDEG + at + 128, columns] = low
                else:
                    for b in range(2):
                        tail_ref[eo, b * LDEG + at:b * LDEG + at + 128, :128] = high
                        tail_ref[eo, b * LDEG + at:b * LDEG + at + 128, 128:] = low


OFFSETS = [(dy, dx) for dy in range(SIDE) for dx in range(SIDE) if (dy, dx) != (0, 0)]


def exchange_kernel(order_ref, coded_ref, got_ref, edge_ref, main_ref, tail_ref, own_sem, send_sem, recv_sem, up_send, up_recv, down_send, down_recv):
    me = lax.axis_index("ord")
    y, x = me // SIDE, me % SIDE
    rad = lax.axis_index("rad")
    count = lax.axis_size("rad")
    upper, lower = (rad + 1) % count, (rad + count - 1) % count

    def other(dy, dx):
        return (y + dy) % SIDE * SIDE + (x + dx) % SIDE

    barrier = pltpu.get_barrier_semaphore()
    for dy, dx in OFFSETS:
        pl.semaphore_signal(barrier, inc=1, device_id={"ord": other(dy, dx)}, device_id_type=MESH)
    for neighbour in (lower, upper):
        pl.semaphore_signal(barrier, inc=1, device_id={"rad": neighbour}, device_id_type=MESH)
    pl.semaphore_wait(barrier, len(OFFSETS) + 2)

    sends = []
    for n, (dy, dx) in enumerate(OFFSETS):
        peer = other(dy, dx)
        copy = pltpu.make_async_remote_copy(
            src_ref=coded_ref.at[peer], dst_ref=got_ref.at[me], send_sem=send_sem.at[n], recv_sem=recv_sem.at[n],
            device_id={"ord": peer}, device_id_type=MESH,
        )
        copy.start()
        sends.append(copy)
    own = pltpu.make_async_copy(coded_ref.at[me], got_ref.at[me], own_sem)
    own.start()
    passed = []

    def pass_on(block, source, n):
        down = pltpu.make_async_remote_copy(
            src_ref=block.at[0:EDGE], dst_ref=edge_ref.at[1, source], send_sem=down_send.at[n], recv_sem=down_recv.at[n],
            device_id={"rad": lower}, device_id_type=MESH,
        )
        up = pltpu.make_async_remote_copy(
            src_ref=block.at[SCALE_ROW:SCALE_ROW + EDGE], dst_ref=edge_ref.at[0, source], send_sem=up_send.at[n], recv_sem=up_recv.at[n],
            device_id={"rad": upper}, device_id_type=MESH,
        )
        down.start()
        up.start()
        passed.extend([down, up])

    pass_on(coded_ref.at[me], me, len(OFFSETS))
    wave_tables(order_ref, main_ref, tail_ref)
    for n, (dy, dx) in enumerate(OFFSETS):
        sends[n].wait_recv()
        source = other(SIDE - dy, SIDE - dx)
        pass_on(got_ref.at[source], source, n)
    own.wait()
    for copy in sends:
        copy.wait_send()
    for copy in passed:
        copy.wait()


def fourier_kernel(got_ref, edge_ref, main_ref, tail_ref, out_ref, middle, edges, inner, outer):
    p = pl.program_id(0)

    @pl.when(p == 0)
    def _():
        rad = lax.axis_index("rad")
        count = lax.axis_size("rad")
        keep_low = jnp.where(rad == 0, 0.0, 1.0) * (1.0 / 0.9999)
        keep_high = jnp.where(rad == count - 1, 0.0, 1.0) * (1.0 / 0.9999)

        def value(coded):
            return coded.astype(jnp.int32).astype(F32)

        for s in range(ORD):
            unit = jnp.exp(LN2 * value(got_ref[s, SCALE_ROW])) * (1.0 / 0.9999)
            for k in range(4):
                at = (k * ORD + s) * LAT
                middle[at:at + LAT, :] = value(got_ref[s, 5 + k]) * unit
            below = jnp.exp(LN2 * value(edge_ref[0, s, 0])) * keep_low
            above = jnp.exp(LN2 * value(edge_ref[1, s, SCALE_ROW])) * keep_high
            for k in range(2):
                at = (k * ORD + s) * LAT
                edges[0, at:at + LAT, :] = value(got_ref[s, k]) * unit
                edges[1, at:at + LAT, :] = value(got_ref[s, EDGE + k]) * unit
                edges[2, at:at + LAT, :] = value(edge_ref[0, s, 1 + k]) * below
                edges[3, at:at + LAT, :] = value(edge_ref[1, s, k]) * above
        mirror = lax.axis_index("ord") >= ORD // 2
        lane = lax.broadcasted_iota(jnp.int32, (32, 128), 1)

        def one(i, _):
            at = jnp.where(mirror, LAT - 1 - i, i)
            mid = middle[pl.ds(at, 64, stride=LAT), :]
            mid = jnp.concatenate([mid, pltpu.roll(mid, 64, 1)], axis=0)
            parts = [edges[e, pl.ds(at, 32, stride=LAT), :] for e in range(4)]
            near, far = [], []
            for q in range(4):
                def shifted(e, place):
                    amount = (place - 32 * q) % 128
                    return pltpu.roll(parts[e], amount, 1) if amount else parts[e]
                near.append(jnp.where(lane < 64, mid[32 * q:32 * q + 32], jnp.where(lane < 96, shifted(0, 64), shifted(1, 96))))
                far.append(jnp.where(lane < 32, shifted(2, 0), shifted(3, 32)))
            inner[pl.ds(i, 128, stride=LAT), :] = jnp.concatenate(near, axis=0).T
            outer[pl.ds(i, 64, stride=LAT), :] = jnp.concatenate(far, axis=0).T[:64]
            return 0

        lax.fori_loop(0, LAT, one, 0)

    def level(eo, c, r):
        tail = 2 * p + c
        if r < 0:
            ref, at = outer, eo * 16 + (r + 2) * 8
        elif r < 2:
            ref, at = inner, 64 + eo * 16 + r * 8
        elif r < 6:
            ref, at = inner, eo * 32 + (r - 2) * 8
        elif r < 8:
            ref, at = inner, 96 + eo * 16 + (r - 6) * 8
        else:
            ref, at = outer, 32 + eo * 16 + (r - 8) * 8
        return ref[pl.ds(pl.multiple_of((at + tail) * LAT, 8), LAT), :]

    totals = []
    for eo in range(2):
        parts = [jnp.concatenate([level(eo, c, r) for r in range(-2, LEV + 2)], axis=0) for c in range(2)]
        high, low = split(jnp.concatenate(parts, axis=1))
        main = jnp.dot(jnp.concatenate([high, low, high], axis=1), main_ref[eo], preferred_element_type=F32)
        tail = jnp.dot(jnp.concatenate([high, low], axis=1), tail_ref[eo], preferred_element_type=F32)
        totals.append(jnp.concatenate([main, tail[:, :128] + tail[:, 128:]], axis=1))
    for side in range(2):
        total = totals[0] + totals[1] if side == 0 else totals[0] - totals[1]
        columns = pl.ds(side * HALF, HALF)
        for r in range(LEV):
            level_of = [total[(r + d) * LAT:(r + d + 1) * LAT] for d in range(5)]
            out_ref[0, 0, r, :, columns] = level_of[2].astype(BF16)
            slope = (level_of[0] - level_of[4]) * (1.0 / 12.0) + (level_of[3] - level_of[1]) * (8.0 / 12.0)
            out_ref[0, 1, r, :, columns] = slope.astype(BF16)


def body(coefficients, order_of_slot):
    own = jnp.transpose(coefficients, (2, 0, 3, 1, 4)).reshape(SLOTS, 64, LDEG)
    vmem = pl.BlockSpec(memory_space=pltpu.VMEM)
    anywhere = pl.BlockSpec(memory_space=pl.ANY)
    coded = pl.pallas_call(
        legendre_kernel,
        out_shape=jax.ShapeDtypeStruct((ORD, ROWS, LAT, 128), jnp.int16),
        in_specs=[pl.BlockSpec(memory_space=pltpu.SMEM), vmem],
        out_specs=vmem,
        scratch_shapes=[
            pltpu.VMEM((3, LDEG * 8, 128), F32),
            pltpu.VMEM((3, SLOTS * 64, 128), F32),
        ],
    )(order_of_slot, own)
    peers = len(OFFSETS)
    got, edge, main, tail = pl.pallas_call(
        exchange_kernel,
        out_shape=[
            jax.ShapeDtypeStruct((ORD, ROWS, LAT, 128), jnp.int16),
            jax.ShapeDtypeStruct((2, ORD, EDGE, LAT, 128), jnp.int16),
            jax.ShapeDtypeStruct((2, 3 * LDEG, 256), BF16),
            jax.ShapeDtypeStruct((2, 2 * LDEG, 256), BF16),
        ],
        in_specs=[vmem, anywhere],
        out_specs=[anywhere, anywhere, vmem, vmem],
        scratch_shapes=[
            pltpu.SemaphoreType.DMA,
            pltpu.SemaphoreType.DMA((peers,)),
            pltpu.SemaphoreType.DMA((peers,)),
            pltpu.SemaphoreType.DMA((ORD,)),
            pltpu.SemaphoreType.DMA((ORD,)),
            pltpu.SemaphoreType.DMA((ORD,)),
            pltpu.SemaphoreType.DMA((ORD,)),
        ],
        compiler_params=pltpu.CompilerParams(collective_id=0, has_side_effects=True),
    )(order_of_slot.reshape(1, LDEG), coded)
    return pl.pallas_call(
        fourier_kernel,
        out_shape=jax.ShapeDtypeStruct((POT, 2, LEV, LAT, NLON), BF16),
        grid=(POT,),
        in_specs=[
            pl.BlockSpec((ORD, ROWS, LAT, 128), lambda p: (0, 0, 0, 0)),
            pl.BlockSpec((2, ORD, EDGE, LAT, 128), lambda p: (0, 0, 0, 0, 0)),
            pl.BlockSpec((2, 3 * LDEG, 256), lambda p: (0, 0, 0)),
            pl.BlockSpec((2, 2 * LDEG, 256), lambda p: (0, 0, 0)),
        ],
        out_specs=pl.BlockSpec((1, 2, LEV, LAT, NLON), lambda p: (p, 0, 0, 0, 0)),
        scratch_shapes=[
            pltpu.VMEM((64 * LAT, 128), F32),
            pltpu.VMEM((4, 32 * LAT, 128), F32),
            pltpu.VMEM((128 * LAT, 128), F32),
            pltpu.VMEM((64 * LAT, 128), F32),
        ],
    )(got, edge, main, tail)


def solution(mesh):
    return jax.shard_map(
        body,
        mesh=mesh,
        in_specs=(P(None, "rad", "ord", None, None), P()),
        out_specs=P(None, None, "rad", "ord", None),
        check_vma=False,
    )
```

time: 61.9 us -> 54.1 us (0.87)
  the two profiles are of different devices: /device:TPU:128 before, /device:TPU:6 now
where the time goes in v2:
time: 54.1 us; the launch traced here: 53.9 us
  Pallas kernels  51.5 us (95%)
  local copies, waits for them, and re-layouts  2.39 us (4%)
    pallas_call x1, Pallas kernels, body(): pl.pallas_call(exchange_kernel, out_shape=[jax.ShapeDtypeStruct((ORD, ROW...  31 us
    pallas_call x1, Pallas kernels, body(): pl.pallas_call(legendre_kernel, out_shape=jax.ShapeDtypeStruct((ORD, ROWS...  10.3 us
    pallas_call x1, Pallas kernels, body(): pl.pallas_call(fourier_kernel, out_shape=jax.ShapeDtypeStruct((POT, 2, LE...  10.2 us
    transpose x1, local copies, waits for them, and re-layouts, body(): own = jnp.transpose(coefficients, (2, 0, 3, 1, 4)).reshape(SLOTS, 64, LDEG)  2.39 us

profile of v2, /device:TPU:6, one launch (start us, length us, event | category | flops | bytes accessed | tf_op | source)
XLA Modules:
  0.0 53.9 jit_solution(12566804263875913838)
XLA Ops:
  0.0 2.4 %copy.3 = bf16[16,4,2,8,256]{4,3,2,1,0:T(8,128)(2,1)} copy(bf16[16,4,2,8,256]{4,2,0,3,1:T(2,128)(2,1)} %bitcast.4) | data formatting | bytes 1048576 | tf_op jit(solution)/shard_map/transpose | solution.py:335
  2.4 10.3 %shard_map.28.coded_ref = s16[16,9,24,128]{3,2,1,0:T(8,128)(2,1)} custom-call(s32[256]{0:T(256)} %order_ref.1, bf16[16,64,256]{2,1,0:T(8,128)(2,1)} %bitcast.3), custom_call_target="tpu_custom_call" | custom-call | tf_op jit(solution)/shard_map/pallas_call | solution.py:338
  12.7 31.0 %shard_map.29 = (s16[16,9,24,128]{3,2,1,0:T(8,128)(2,1)}, s16[2,16,3,24,128]{4,3,2,1,0:T(8,128)(2,1)}, bf16[2,768,256]{2,1,0:T(8,128)(2,1)}, bf16[2,512,256]{2,1,0:T(8,128)(2,1)}) custom-call(s32[1,256]{1,0:T(1,128)} %bitcast.5, s16[16,9,24,128]{3,2,1,0:T(8,128)(2,1)} %shard_map.28.coded_ref), custom_call_target="tpu_custom_call" | custom-call | tf_op jit(solution)/shard_map/pallas_call | solution.py:349
  43.7 10.2 %shard_map.30 = bf16[4,2,8,24,768]{4,3,2,1,0:T(8,128)(2,1)} custom-call(s16[16,9,24,128]{3,2,1,0:T(8,128)(2,1)} %get-tuple-element.9.got_ref, s16[2,16,3,24,128]{4,3,2,1,0:T(8,128)(2,1)} %get-tuple-element.10.edge_ref, bf16[2,768,256]{2,1,0:T(8,128)(2,1)} %get-tuple-element.11.main_ref, bf16[2,512,256]{2,1,0:T(8,128)(2,1)} %get-tuple-element.12.tail_ref), custom_call_target="tpu_custom_call" | custom-call | tf_op jit(solution)/shard_map/pallas_call | solution.py:370

commit v3 on v2

v3 whole, which is shorter than its diff:
```python
import math

import jax
import jax.numpy as jnp
from jax import lax
from jax.experimental import pallas as pl
from jax.experimental.pallas import tpu as pltpu
from jax.sharding import PartitionSpec as P

LDEG = 256
NLAT = 384
NLON = 768
HALF = NLON // 2
POT = 4
LEV = 8
SLOTS = 16
PAIRS = 8
ORD = 16
SIDE = 4
LAT = NLAT // ORD
NORTH = NLAT // 2
UNITS = 25
SCALE = 6
EDGE = 7
FIRST = (0, 3, 7, 10, 13, 16, 19, 22)
STEP = 32
GROUP = 6
LOOP = True
LN2 = math.log(2.0)
F32 = jnp.float32
BF16 = jnp.bfloat16
MESH = pl.DeviceIdType.MESH


def split(x):
    high = x.astype(BF16)
    return high, (x - high.astype(F32)).astype(BF16)


def legendre(order_ref, own_ref, ready_copies, out_ref, fresh, spare, high_table, low_table, sums):
    first = lax.axis_index("ord") * SLOTS
    slots, orders = [0] * SLOTS, [0] * SLOTS
    for g in range(PAIRS):
        head = order_ref[first + 2 * g]
        odd = head & 1
        even_order = jnp.where(odd == 0, head, LDEG - 1 - head)
        slots[g], slots[PAIRS + g] = 2 * g + odd, 2 * g + 1 - odd
        orders[g], orders[PAIRS + g] = even_order, LDEG - 1 - even_order
    row = lax.broadcasted_iota(jnp.int32, (SLOTS, 128), 0)
    order = jnp.zeros((SLOTS, 128), jnp.int32)
    for i in range(SLOTS):
        order = jnp.where(row == i, orders[i], order)
    m = jnp.concatenate([order, order], axis=1).astype(F32)
    degree = lax.broadcasted_iota(jnp.int32, (SLOTS, LDEG), 1).astype(F32)
    msq = m * m
    raising = jnp.sqrt(jnp.maximum(4.0 * degree * degree - 1.0, 1.0) / jnp.maximum(degree * degree - msq, 1.0))
    below = degree - 1.0
    lowering = jnp.sqrt(jnp.maximum(below * below - msq, 0.0) / jnp.maximum(4.0 * below * below - 1.0, 1.0))
    lowering = raising * lowering
    factor = jnp.maximum(degree, 1.0)
    logs = jnp.log((2.0 * factor - 1.0) / (2.0 * factor))
    logs = jnp.where((degree >= 1.0) & (degree <= m), logs, 0.0)
    product = jnp.sum(logs, axis=1, keepdims=True)
    base = 0.5 * jnp.log((2.0 * m[:, :128] + 1.0) / (4.0 * math.pi)) + 0.5 * product

    lane = lax.broadcasted_iota(jnp.int32, (8, 128), 1)
    half = lane < 64

    def tiles(x):
        return [x[:8, :128], x[8:, :128], jnp.where(half, x[:8, :128], x[8:, :128])]

    theta = [math.pi * (lane.astype(F32) + 0.5) / NLAT, math.pi * ((lane & 63).astype(F32) + 128.5) / NLAT]
    cosine = [jnp.cos(t) for t in theta]
    log_sine = [jnp.log(jnp.sin(t)) for t in theta]
    cosine = [cosine[0], cosine[0], cosine[1]]
    log_sine = [log_sine[0], log_sine[0], log_sine[1]]
    order_tiles = tiles(order)
    start_scale = [b + k * s for b, k, s in zip(tiles(base), tiles(m), log_sine)]

    spare[...] = jnp.zeros_like(spare)

    def refine(stage, t, s, at):
        values = stage[t, pl.ds(s, STEP, stride=8), :]
        high, low = split(values)
        high_table[t, s, pl.ds(at, STEP), :] = high
        low_table[t, s, pl.ds(at, STEP), :] = low

    def block(step, carry):
        last, prior, scale = [list(c) for c in carry]
        for side, (stage, ready) in enumerate(((fresh, spare), (spare, fresh))):
            start = (2 * step + side) * STEP
            at = pl.multiple_of(start, STEP)
            up = pltpu.roll(raising, LDEG - start, 1)
            down = pltpu.roll(lowering, LDEG - start, 1)
            jobs = [(t, s) for t in range(3) for s in range(PAIRS)]
            for j in range(STEP):
                if j % 8 == 0:
                    growth = [jnp.exp(s) for s in scale]
                ups = tiles(jnp.broadcast_to(up[:, j:j + 1], (SLOTS, 128)))
                downs = tiles(jnp.broadcast_to(down[:, j:j + 1], (SLOTS, 128)))
                for t in range(3):
                    seed = jnp.where(order_tiles[t] == start + j, 1.0, 0.0)
                    new = (ups[t] * cosine[t]) * last[t] + (seed - downs[t] * prior[t])
                    stage[t, 8 * j:8 * j + 8, :] = new * growth[t]
                    last[t], prior[t] = new, last[t]
                if j % 8 == 7:
                    for t in range(3):
                        large = jnp.abs(last[t]) > 1e10
                        shrink = jnp.where(large, 1e-10, 1.0)
                        last[t], prior[t] = last[t] * shrink, prior[t] * shrink
                        scale[t] = scale[t] + jnp.where(large, 10.0 * math.log(10.0), 0.0)
                while jobs and len(jobs) * STEP > 24 * (STEP - 1 - j):
                    t, s = jobs.pop()
                    refine(ready, t, s, at)
        return tuple(last), tuple(prior), tuple(scale)

    blank = tuple(jnp.zeros((8, 128), F32) for _ in range(3))
    lax.fori_loop(0, LDEG // (2 * STEP), block, (blank, blank, tuple(start_scale)))
    for t in range(3):
        for s in range(PAIRS):
            refine(spare, t, s, LDEG)

    parity = lax.broadcasted_iota(jnp.int32, (64, LDEG), 1) & 1
    parity = parity.astype(F32).astype(BF16)
    wide = lax.broadcasted_iota(jnp.int32, (64, 128), 1) < 64
    for copy in ready_copies:
        copy.wait()
    top = [jnp.zeros((8, 128), F32) for _ in range(3)]
    body_rows = slice(STEP, STEP + LDEG)
    for g in range(PAIRS):
        for eo in range(2):
            left = own_ref[slots[eo * PAIRS + g]].reshape(64, LDEG)
            odd_left = left * parity
            left = jnp.concatenate([left - odd_left, odd_left], axis=0)
            right = jnp.concatenate(
                [jnp.concatenate([table[eo, g, body_rows], table[2, g, body_rows]], axis=1) for table in (high_table, low_table)],
                axis=0,
            )
            got = jnp.dot(jnp.concatenate([left, left], axis=1), right, preferred_element_type=F32)
            north = got[:64] + got[64:]
            south = got[:64] - got[64:] if eo == 0 else got[64:] - got[:64]
            near, far = north[:, 128:], south[:, 128:]
            if eo == 0:
                mixed = jnp.where(wide, near, pltpu.roll(far, 64, 1))
            else:
                mixed = jnp.where(wide, pltpu.roll(near, 64, 1), far)
            at = (2 * g + eo) * 64
            for t, part in enumerate((north[:, :128], south[:, :128], mixed)):
                sums[t, at:at + 64, :] = part
                top[t] = jnp.maximum(top[t], jnp.max(jnp.abs(part.reshape(8, 8, 128)), axis=0))

    powers = []
    for t in range(3):
        peak = jnp.max(top[t], axis=0, keepdims=True)
        power = jnp.ceil(jnp.log(jnp.maximum(peak, 1e-30)) * (1.0 / LN2) + 0.001) - 15.0
        inverse = jnp.broadcast_to(jnp.exp(-LN2 * power) * 0.9999, (128, 128))
        powers.append(power)
        for k in range(8):
            if k < 2:
                picks = [(2 * q + k, eo, r) for q in range(4) for eo in range(2) for r in (0, 1)]
            elif k < 4:
                picks = [(2 * q + k - 2, eo, r) for q in range(4) for eo in range(2) for r in (6, 7)]
            else:
                picks = [(4 * h + k - 4, eo, r) for h in range(2) for eo in range(2) for r in (2, 3, 4, 5)]
            pieces = [sums[t, (2 * g + eo) * 64 + 8 * r:(2 * g + eo) * 64 + 8 * r + 8, :] for g, eo, r in picks]
            coded = jnp.round(jnp.concatenate(pieces, axis=0) * inverse)
            coded = coded.T.astype(jnp.int32)
            if t < 2:
                spans = [(d, 0, 3, LAT * d) for d in range(5)] + [(5, 0, 1, 120)]
                spans = [(d if t == 0 else ORD - 1 - d, lo, hi, at) for d, lo, hi, at in spans]
            else:
                spans = [(5, 1, 3, 0), (6, 0, 3, 16), (7, 0, 3, 40)]
                spans = spans + [(ORD - 1 - d, lo, hi, at + 64) for d, lo, hi, at in spans]
            for d, lo, hi, at in spans:
                part = coded[at:at + 8 * (hi - lo)].reshape(hi - lo, 8, 128)
                out_ref[d, FIRST[k] + lo:FIRST[k] + hi] = part.astype(jnp.int16)
    sublane = lax.broadcasted_iota(jnp.int32, (8, 128), 0)
    power = jnp.where(sublane == 0, powers[0], jnp.where(sublane == 1, powers[1], powers[2]))
    power = power.astype(jnp.int32).astype(jnp.int16)
    for d in range(ORD):
        out_ref[d, SCALE] = power


def turn(product):
    rest = product - NLON * jnp.floor(product * (1.0 / NLON))
    quarter = jnp.floor(rest * (1.0 / 192.0) + 0.5)
    x = (rest - 192.0 * quarter) * (2.0 * math.pi / NLON)
    y = x * x
    sine = x * (1.0 + y * (-1.0 / 6.0 + y * (1.0 / 120.0 + y * (-1.0 / 5040.0 + y * (1.0 / 362880.0)))))
    cosine = 1.0 + y * (-0.5 + y * (1.0 / 24.0 + y * (-1.0 / 720.0 + y * (1.0 / 40320.0 - y * (1.0 / 3628800.0)))))
    swap = (quarter == 1.0) | (quarter == 3.0)
    first = jnp.where(swap, sine, cosine)
    second = jnp.where(swap, cosine, sine)
    first = jnp.where((quarter == 1.0) | (quarter == 2.0), -first, first)
    second = jnp.where((quarter == 2.0) | (quarter == 3.0), -second, second)
    return first, second


def wave_tables(order_ref, main_ref, tail_ref):
    row = lax.broadcasted_iota(jnp.int32, (128, LDEG), 0)
    lane = lax.broadcasted_iota(jnp.int32, (128, LDEG), 1)
    source = (row & 15) * SLOTS + 2 * (row >> 4)
    heads = jnp.broadcast_to(order_ref[...], (128, LDEG)).astype(F32)
    head = jnp.sum(jnp.where(lane == source, heads, 0.0), axis=1, keepdims=True)
    even = jnp.where(head - 2.0 * jnp.floor(0.5 * head) == 0.0, head, LDEG - 1 - head)
    for eo in range(2):
        order = jnp.broadcast_to(even if eo == 0 else LDEG - 1 - even, (128, 128))
        weight = jnp.where(order == 0.0, 1.0, 2.0)
        for j in range(3):
            k = lax.broadcasted_iota(jnp.int32, (128, 128), 1).astype(F32) + 128.0 * j
            cosine, sine = turn(order * k)
            for c, wave in enumerate((weight * cosine, -weight * sine)):
                high, low = split(wave)
                at = c * 128
                if j < 2:
                    columns = pl.ds(128 * j, 128)
                    main_ref[eo, at:at + 128, columns] = high
                    main_ref[eo, LDEG + at:LDEG + at + 128, columns] = high
                    main_ref[eo, 2 * LDEG + at:2 * LDEG + at + 128, columns] = low
                else:
                    for b in range(2):
                        tail_ref[eo, b * LDEG + at:b * LDEG + at + 128, :128] = high
                        tail_ref[eo, b * LDEG + at:b * LDEG + at + 128, 128:] = low


OFFSETS = [(dy, dx) for dy in range(SIDE) for dx in range(SIDE) if (dy, dx) != (0, 0)]
OFFSETS.sort(key=lambda o: -min(o[0], SIDE - o[0]) - min(o[1], SIDE - o[1]))


def exchange_kernel(
    order_ref, heads_ref, coefficients_ref, got_ref, edge_ref, main_ref, tail_ref,
    own_ref, coded_ref, fresh, spare, high_table, low_table, sums,
    load_sem, own_sem, send_sem, recv_sem, up_send, up_recv, down_send, down_recv,
):
    me = lax.axis_index("ord")
    y, x = me // SIDE, me % SIDE
    rad = lax.axis_index("rad")
    count = lax.axis_size("rad")
    upper, lower = (rad + 1) % count, (rad + count - 1) % count

    def other(dy, dx):
        return (y + dy) % SIDE * SIDE + (x + dx) % SIDE

    barrier = pltpu.get_barrier_semaphore()
    for dy, dx in OFFSETS:
        pl.semaphore_signal(barrier, inc=1, device_id={"ord": other(dy, dx)}, device_id_type=MESH)
    for neighbour in (lower, upper):
        pl.semaphore_signal(barrier, inc=1, device_id={"rad": neighbour}, device_id_type=MESH)

    loads = []
    for p in range(POT):
        for r in range(LEV):
            copy = pltpu.make_async_copy(coefficients_ref.at[p, r], own_ref.at[:, r, p], load_sem.at[p * LEV + r])
            copy.start()
            loads.append(copy)
    legendre(order_ref, own_ref, loads, coded_ref, fresh, spare, high_table, low_table, sums)
    pl.semaphore_wait(barrier, len(OFFSETS) + 2)

    sends = []
    for n, (dy, dx) in enumerate(OFFSETS):
        peer = other(dy, dx)
        copy = pltpu.make_async_remote_copy(
            src_ref=coded_ref.at[peer], dst_ref=got_ref.at[me], send_sem=send_sem.at[n], recv_sem=recv_sem.at[n],
            device_id={"ord": peer}, device_id_type=MESH,
        )
        copy.start()
        sends.append(copy)
    own = pltpu.make_async_copy(coded_ref.at[me], got_ref.at[me], own_sem)
    own.start()
    passed = []

    def pass_on(block, source, n):
        down = pltpu.make_async_remote_copy(
            src_ref=block.at[0:EDGE], dst_ref=edge_ref.at[1, source], send_sem=down_send.at[n], recv_sem=down_recv.at[n],
            device_id={"rad": lower}, device_id_type=MESH,
        )
        up = pltpu.make_async_remote_copy(
            src_ref=block.at[SCALE:SCALE + EDGE], dst_ref=edge_ref.at[0, source], send_sem=up_send.at[n], recv_sem=up_recv.at[n],
            device_id={"rad": upper}, device_id_type=MESH,
        )
        down.start()
        up.start()
        passed.extend([down, up])

    pass_on(coded_ref.at[me], me, len(OFFSETS))
    wave_tables(heads_ref, main_ref, tail_ref)
    for n, (dy, dx) in enumerate(OFFSETS):
        sends[n].wait_recv()
        source = other(SIDE - dy, SIDE - dx)
        pass_on(got_ref.at[source], source, n)
    own.wait()
    for copy in sends:
        copy.wait_send()
    for copy in passed:
        copy.wait()


def fourier_kernel(got_ref, edge_ref, main_ref, tail_ref, out_ref, middle, edges, scales, turned, inner, outer, result, sem):
    rad = lax.axis_index("rad")
    count = lax.axis_size("rad")
    keep_low = jnp.where(rad == 0, 0.0, 1.0) * (1.0 / 0.9999)
    keep_high = jnp.where(rad == count - 1, 0.0, 1.0) * (1.0 / 0.9999)
    place = lax.axis_index("ord")
    mirror = place >= ORD // 2
    first = jnp.where(mirror, ORD - 1 - place, place) * LAT

    def value(coded):
        return coded.astype(jnp.int32).astype(F32)

    def take(coded):
        return value(coded).reshape(LAT, 128)

    for s in range(ORD):
        for k in range(4):
            at = (k * ORD + s) * LAT
            middle[at:at + LAT, :] = take(got_ref[s, 13 + 3 * k:16 + 3 * k])
        for k in range(2):
            at = (k * ORD + s) * LAT
            edges[0, at:at + LAT, :] = take(got_ref[s, 3 * k:3 * k + 3])
            edges[1, at:at + LAT, :] = take(got_ref[s, 7 + 3 * k:10 + 3 * k])
            edges[2, at:at + LAT, :] = take(edge_ref[0, s, 1 + 3 * k:4 + 3 * k])
            edges[3, at:at + LAT, :] = take(edge_ref[1, s, 3 * k:3 * k + 3])
        scales[0, 8 * s:8 * s + 8, :] = value(got_ref[s, SCALE])
        scales[1, 8 * s:8 * s + 8, :] = value(edge_ref[0, s, 0])
        scales[2, 8 * s:8 * s + 8, :] = value(edge_ref[1, s, SCALE])
    for e in range(3):
        for t in range(3):
            row = scales[e, pl.ds(t, ORD, stride=8), :]
            turned[e, 128 * t:128 * t + 128, :] = jnp.concatenate([row] * 8, axis=0).T

    lane = lax.broadcasted_iota(jnp.int32, (32, 128), 1)

    def one(i):
        at = jnp.where(mirror, LAT - 1 - i, i)
        north = first + at
        row = jnp.where(north < 128, north + jnp.where(mirror, 128, 0), north + 128 + jnp.where(mirror, 64, 0))
        unit = [jnp.exp(LN2 * turned[e, pl.ds(row, 1), :]) for e in range(3)]
        mid = middle[pl.ds(at, 64, stride=LAT), :]
        mid = jnp.concatenate([mid, pltpu.roll(mid, 64, 1)], axis=0)
        parts = [edges[e, pl.ds(at, 32, stride=LAT), :] for e in range(4)]
        near, far = [], []
        for q in range(4):
            def shifted(e, target):
                amount = (target - 32 * q) % 128
                return pltpu.roll(parts[e], amount, 1) if amount else parts[e]
            near.append(jnp.where(lane < 64, mid[32 * q:32 * q + 32], jnp.where(lane < 96, shifted(0, 64), shifted(1, 96))))
            far.append(jnp.where(lane < 32, shifted(2, 0), shifted(3, 32)))
        far = jnp.concatenate(far, axis=0).T
        inner[pl.ds(i, 128, stride=LAT), :] = jnp.concatenate(near, axis=0).T * (unit[0] * (1.0 / 0.9999))
        outer[pl.ds(i, 32, stride=LAT), :] = far[:32] * (unit[1] * keep_low)
        outer[pl.ds(32 * LAT + i, 32, stride=LAT), :] = far[32:64] * (unit[2] * keep_high)

    @pl.loop(0, LAT // GROUP)
    def _(n):
        for i in range(GROUP):
            one(n * GROUP + i)

    def level(eo, c, p, r):
        tail = 2 * p + c
        if r < 0:
            ref, at = outer, eo * 16 + (r + 2) * 8
        elif r < 2:
            ref, at = inner, 64 + eo * 16 + r * 8
        elif r < 6:
            ref, at = inner, eo * 32 + (r - 2) * 8
        elif r < 8:
            ref, at = inner, 96 + eo * 16 + (r - 6) * 8
        else:
            ref, at = outer, 32 + eo * 16 + (r - 8) * 8
        return ref[pl.ds(pl.multiple_of((at + tail) * LAT, 8), LAT), :]

    def potential(p):
        totals = []
        for eo in range(2):
            parts = [jnp.concatenate([level(eo, c, p, r) for r in range(-2, LEV + 2)], axis=0) for c in range(2)]
            high, low = split(jnp.concatenate(parts, axis=1))
            main = jnp.dot(jnp.concatenate([high, low, high], axis=1), main_ref[eo], preferred_element_type=F32)
            tail = jnp.dot(jnp.concatenate([high, low], axis=1), tail_ref[eo], preferred_element_type=F32)
            totals.append(jnp.concatenate([main, tail[:, :128] + tail[:, 128:]], axis=1))
        for side in range(2):
            total = totals[0] + totals[1] if side == 0 else totals[0] - totals[1]
            columns = pl.ds(side * HALF, HALF)
            for r in range(LEV):
                level_of = [total[(r + d) * LAT:(r + d + 1) * LAT] for d in range(5)]
                result[p, 0, r, :, columns] = level_of[2].astype(BF16)
                slope = (level_of[0] - level_of[4]) * (1.0 / 12.0) + (level_of[3] - level_of[1]) * (8.0 / 12.0)
                result[p, 1, r, :, columns] = slope.astype(BF16)
        pltpu.make_async_copy(result.at[p], out_ref.at[p], sem.at[p]).start()

    if LOOP:
        @pl.loop(0, POT)
        def _(p):
            potential(p)
    else:
        for p in range(POT):
            potential(p)
    for p in range(POT):
        pltpu.make_async_copy(result.at[p], out_ref.at[p], sem.at[p]).wait()


def body(coefficients, order_of_slot):
    vmem = pl.BlockSpec(memory_space=pltpu.VMEM)
    anywhere = pl.BlockSpec(memory_space=pl.ANY)
    peers = len(OFFSETS)
    got, edge, main, tail = pl.pallas_call(
        exchange_kernel,
        out_shape=[
            jax.ShapeDtypeStruct((ORD, UNITS, 8, 128), jnp.int16),
            jax.ShapeDtypeStruct((2, ORD, EDGE, 8, 128), jnp.int16),
            jax.ShapeDtypeStruct((2, 3 * LDEG, 256), BF16),
            jax.ShapeDtypeStruct((2, 2 * LDEG, 256), BF16),
        ],
        in_specs=[pl.BlockSpec(memory_space=pltpu.SMEM), vmem, anywhere],
        out_specs=[anywhere, anywhere, vmem, vmem],
        scratch_shapes=[
            pltpu.VMEM((SLOTS, LEV, POT, 2, LDEG), BF16),
            pltpu.VMEM((ORD, UNITS, 8, 128), jnp.int16),
            pltpu.VMEM((3, PAIRS * STEP, 128), F32),
            pltpu.VMEM((3, PAIRS * STEP, 128), F32),
            pltpu.VMEM((3, PAIRS, STEP + LDEG, 128), BF16),
            pltpu.VMEM((3, PAIRS, STEP + LDEG, 128), BF16),
            pltpu.VMEM((3, SLOTS * 64, 128), F32),
            pltpu.SemaphoreType.DMA((POT * LEV,)),
            pltpu.SemaphoreType.DMA,
            pltpu.SemaphoreType.DMA((peers,)),
            pltpu.SemaphoreType.DMA((peers,)),
            pltpu.SemaphoreType.DMA((ORD,)),
            pltpu.SemaphoreType.DMA((ORD,)),
            pltpu.SemaphoreType.DMA((ORD,)),
            pltpu.SemaphoreType.DMA((ORD,)),
        ],
        compiler_params=pltpu.CompilerParams(collective_id=0, has_side_effects=True),
    )(order_of_slot, order_of_slot.reshape(1, LDEG), coefficients)
    return pl.pallas_call(
        fourier_kernel,
        out_shape=jax.ShapeDtypeStruct((POT, 2, LEV, LAT, NLON), BF16),
        in_specs=[vmem] * 4,
        out_specs=anywhere,
        scratch_shapes=[
            pltpu.VMEM((64 * LAT, 128), F32),
            pltpu.VMEM((4, 32 * LAT, 128), F32),
            pltpu.VMEM((3, 128, 128), F32),
            pltpu.VMEM((3, NLAT, 128), F32),
            pltpu.VMEM((128 * LAT, 128), F32),
            pltpu.VMEM((64 * LAT, 128), F32),
            pltpu.VMEM((POT, 2, LEV, LAT, NLON), BF16),
            pltpu.SemaphoreType.DMA((POT,)),
        ],
    )(got, edge, main, tail)


def solution(mesh):
    return jax.shard_map(
        body,
        mesh=mesh,
        in_specs=(P(None, "rad", "ord", None, None), P()),
        out_specs=P(None, None, "rad", "ord", None),
        check_vma=False,
    )
```

time: 54.1 us -> 40.3 us (0.74)
  Pallas kernels: 51.5 us -> 40 us
  local copies, waits for them, and re-layouts: 2.39 us -> 0 us
    pallas_call x2 -> x1, Pallas kernels: 41.3 us -> 31.8 us  [body(): pl.pallas_call(exchange_kernel, out_shape=[jax.ShapeDtypeStruct((ORD, UNI...]
    transpose x1 -> x0, local copies, waits for them, and re-layouts: 2.39 us -> none  [body(): own = jnp.transpose(coefficients, (2, 0, 3, 1, 4)).reshape(SLOTS, 64, LDEG)]
    pallas_call x1, Pallas kernels: 10.2 us -> 8.21 us  [body(): pl.pallas_call(fourier_kernel, out_shape=jax.ShapeDtypeStruct((POT, 2, LE...]
where the time goes in v3:
time: 40.3 us; the launch traced here: 40.1 us
  Pallas kernels  40 us (99%)
    pallas_call x1, Pallas kernels, body(): pl.pallas_call(exchange_kernel, out_shape=[jax.ShapeDtypeStruct((ORD, UNI...  31.8 us
    pallas_call x1, Pallas kernels, body(): pl.pallas_call(fourier_kernel, out_shape=jax.ShapeDtypeStruct((POT, 2, LE...  8.21 us

profile of v3, /device:TPU:6, one launch (start us, length us, event | category | flops | bytes accessed | tf_op | source)
XLA Modules:
  0.0 40.1 jit_solution(10621671602484232099)
XLA Ops:
  0.0 31.8 %shard_map.28 = (s16[16,25,8,128]{3,2,1,0:T(8,128)(2,1)}, s16[2,16,7,8,128]{4,3,2,1,0:T(8,128)(2,1)}, bf16[2,768,256]{2,1,0:T(8,128)(2,1)}, bf16[2,512,256]{2,1,0:T(8,128)(2,1)}) custom-call(s32[256]{0:T(256)} %order_ref.1, s32[1,256]{1,0:T(1,128)} %bitcast.1, bf16[4,8,16,2,256]{4,3,2,1,0:T(2,128)(2,1)} %coefficients_ref.1), custom_call_target="tpu_custom_call" | custom-call | tf_op jit(solution)/shard_map/pallas_call | solution.py:405
  31.9 8.2 %shard_map.29 = bf16[4,2,8,24,768]{4,3,2,1,0:T(8,128)(2,1)} custom-call(s16[16,25,8,128]{3,2,1,0:T(8,128)(2,1)} %get-tuple-element.9.got_ref, s16[2,16,7,8,128]{4,3,2,1,0:T(8,128)(2,1)} %get-tuple-element.10.edge_ref, bf16[2,768,256]{2,1,0:T(8,128)(2,1)} %get-tuple-element.11.main_ref, bf16[2,512,256]{2,1,0:T(8,128)(2,1)} %get-tuple-element.12.tail_ref), custom_call_target="tpu_custom_call" | custom-call | tf_op jit(solution)/shard_map/pallas_call | solution.py:434

commit v4 on v3

--- a/solution.py
+++ b/solution.py
@@ -24,8 +24,7 @@
 EDGE = 7
 FIRST = (0, 3, 7, 10, 13, 16, 19, 22)
 STEP = 32
-GROUP = 6
-LOOP = True
+GROUP = 12
 LN2 = math.log(2.0)
 F32 = jnp.float32
 BF16 = jnp.bfloat16
@@ -227,10 +226,58 @@
 OFFSETS.sort(key=lambda o: -min(o[0], SIDE - o[0]) - min(o[1], SIDE - o[1]))
 
 
+def value(coded):
+    return coded.astype(jnp.int32).astype(F32)
+
+
+def take(coded):
+    return value(coded).reshape(LAT, 128)
+
+
+def place_of_latitudes():
+    place = lax.axis_index("ord")
+    mirror = place >= ORD // 2
+    first = jnp.where(mirror, ORD - 1 - place, place) * LAT
+
+    def place(i):
+        at = jnp.where(mirror, LAT - 1 - i, i)
+        north = first + at
+        row = jnp.where(north < 128, north + jnp.where(mirror, 128, 0), north + 128 + jnp.where(mirror, 64, 0))
+        return at, row
+
+    return place
+
+
+def turn_scales(scales, turned):
+    for t in range(3):
+        row = scales[pl.ds(t, ORD, stride=8), :]
+        turned[128 * t:128 * t + 128, :] = jnp.concatenate([row] * 8, axis=0).T
+
+
+def turner(parts):
+    width = 128 // parts
+    lane = lax.broadcasted_iota(jnp.int32, (width, 256), 1)
+    row = lax.broadcasted_iota(jnp.int32, (width, 256), 0)
+    pick = jnp.where((lane & (width - 1)) == row, 1.0, 0.0).astype(BF16)
+
+    def turn_blocks(blocks):
+        rows = []
+        for block in blocks:
+            high, low = split(block)
+            group = lax.broadcasted_iota(jnp.int32, block.shape, 1) // width
+            for q in range(parts):
+                keep = jnp.where(group == q, 1.0, 0.0).astype(BF16)
+                rows.append(jnp.concatenate([high * keep, low * keep], axis=1))
+        rows = jnp.concatenate(rows, axis=0)
+        return lax.dot_general(pick, rows, (((1,), (1,)), ((), ())), preferred_element_type=F32)
+
+    return turn_blocks
+
+
 def exchange_kernel(
-    order_ref, heads_ref, coefficients_ref, got_ref, edge_ref, main_ref, tail_ref,
-    own_ref, coded_ref, fresh, spare, high_table, low_table, sums,
-    load_sem, own_sem, send_sem, recv_sem, up_send, up_recv, down_send, down_recv,
+    order_ref, heads_ref, coefficients_ref, inner_ref, edge_ref, main_ref, tail_ref,
+    own_ref, coded_ref, fresh, spare, high_table, low_table, sums, got_ref, middle, edges, scales, turned, inner,
+    load_sem, out_sem, send_sem, recv_sem, up_send, up_recv, down_send, down_recv,
 ):
     me = lax.axis_index("ord")
     y, x = me // SIDE, me % SIDE
@@ -265,8 +312,6 @@
         )
         copy.start()
         sends.append(copy)
-    own = pltpu.make_async_copy(coded_ref.at[me], got_ref.at[me], own_sem)
-    own.start()
     passed = []
 
     def pass_on(block, source, n):
@@ -282,78 +327,86 @@
         up.start()
         passed.extend([down, up])
 
+    def unpack(ref, source):
+        for k in range(4):
+            at = pl.multiple_of((k * ORD + source) * LAT, 8)
+            middle[pl.ds(at, LAT), :] = take(ref[source, 13 + 3 * k:16 + 3 * k])
+        for k in range(2):
+            at = pl.multiple_of((k * ORD + source) * LAT, 8)
+            edges[0, pl.ds(at, LAT), :] = take(ref[source, 3 * k:3 * k + 3])
+            edges[1, pl.ds(at, LAT), :] = take(ref[source, 7 + 3 * k:10 + 3 * k])
+        scales[pl.ds(pl.multiple_of(8 * source, 8), 8), :] = value(ref[source, SCALE])
+
     pass_on(coded_ref.at[me], me, len(OFFSETS))
     wave_tables(heads_ref, main_ref, tail_ref)
+    unpack(coded_ref, me)
     for n, (dy, dx) in enumerate(OFFSETS):
         sends[n].wait_recv()
         source = other(SIDE - dy, SIDE - dx)
         pass_on(got_ref.at[source], source, n)
-    own.wait()
+        unpack(got_ref, source)
+    turn_scales(scales, turned)
+    place = place_of_latitudes()
+    turn_middle, turn_edges = turner(2), turner(4)
+
+    @pl.loop(0, LAT // GROUP)
+    def _(n):
+        for j in range(GROUP):
+            i = n * GROUP + j
+            at, row = place(i)
+            unit = jnp.exp(LN2 * turned[pl.ds(row, 1), :]) * (1.0 / 0.9999)
+            mid = turn_middle([middle[pl.ds(at, 64, stride=LAT), :]])
+            ends = turn_edges([edges[e, pl.ds(at, 32, stride=LAT), :] for e in range(2)])
+            inner[pl.ds(i, 64, stride=LAT), :] = mid * unit
+            inner[pl.ds(64 * LAT + i, 32, stride=LAT), :] = ends[:, :128] * unit
+            inner[pl.ds(96 * LAT + i, 32, stride=LAT), :] = ends[:, 128:] * unit
+
+    result = pltpu.make_async_copy(inner, inner_ref, out_sem)
+    result.start()
     for copy in sends:
         copy.wait_send()
     for copy in passed:
         copy.wait()
-
-
-def fourier_kernel(got_ref, edge_ref, main_ref, tail_ref, out_ref, middle, edges, scales, turned, inner, outer, result, sem):
+    result.wait()
+
+
+def fourier_kernel(inner_hbm, edge_hbm, main_hbm, tail_hbm, out_ref, inner, edge_ref, main_ref, tail_ref, edges, scales, turned, outer, result, load_sem, sem):
+    loads = [
+        pltpu.make_async_copy(source, target, load_sem.at[n])
+        for n, (source, target) in enumerate(((edge_hbm, edge_ref), (inner_hbm, inner), (main_hbm, main_ref), (tail_hbm, tail_ref)))
+    ]
+    for copy in loads:
+        copy.start()
+    loads[0].wait()
     rad = lax.axis_index("rad")
     count = lax.axis_size("rad")
     keep_low = jnp.where(rad == 0, 0.0, 1.0) * (1.0 / 0.9999)
     keep_high = jnp.where(rad == count - 1, 0.0, 1.0) * (1.0 / 0.9999)
-    place = lax.axis_index("ord")
-    mirror = place >= ORD // 2
-    first = jnp.where(mirror, ORD - 1 - place, place) * LAT
-
-    def value(coded):
-        return coded.astype(jnp.int32).astype(F32)
-
-    def take(coded):
-        return value(coded).reshape(LAT, 128)
-
     for s in range(ORD):
-        for k in range(4):
-            at = (k * ORD + s) * LAT
-            middle[at:at + LAT, :] = take(got_ref[s, 13 + 3 * k:16 + 3 * k])
         for k in range(2):
             at = (k * ORD + s) * LAT
-            edges[0, at:at + LAT, :] = take(got_ref[s, 3 * k:3 * k + 3])
-            edges[1, at:at + LAT, :] = take(got_ref[s, 7 + 3 * k:10 + 3 * k])
-            edges[2, at:at + LAT, :] = take(edge_ref[0, s, 1 + 3 * k:4 + 3 * k])
-            edges[3, at:at + LAT, :] = take(edge_ref[1, s, 3 * k:3 * k + 3])
-        scales[0, 8 * s:8 * s + 8, :] = value(got_ref[s, SCALE])
-        scales[1, 8 * s:8 * s + 8, :] = value(edge_ref[0, s, 0])
-        scales[2, 8 * s:8 * s + 8, :] = value(edge_ref[1, s, SCALE])
-    for e in range(3):
-        for t in range(3):
-            row = scales[e, pl.ds(t, ORD, stride=8), :]
-            turned[e, 128 * t:128 * t + 128, :] = jnp.concatenate([row] * 8, axis=0).T
-
-    lane = lax.broadcasted_iota(jnp.int32, (32, 128), 1)
-
-    def one(i):
-        at = jnp.where(mirror, LAT - 1 - i, i)
-        north = first + at
-        row = jnp.where(north < 128, north + jnp.where(mirror, 128, 0), north + 128 + jnp.where(mirror, 64, 0))
-        unit = [jnp.exp(LN2 * turned[e, pl.ds(row, 1), :]) for e in range(3)]
-        mid = middle[pl.ds(at, 64, stride=LAT), :]
-        mid = jnp.concatenate([mid, pltpu.roll(mid, 64, 1)], axis=0)
-        parts = [edges[e, pl.ds(at, 32, stride=LAT), :] for e in range(4)]
-        near, far = [], []
-        for q in range(4):
-            def shifted(e, target):
-                amount = (target - 32 * q) % 128
-                return pltpu.roll(parts[e], amount, 1) if amount else parts[e]
-            near.append(jnp.where(lane < 64, mid[32 * q:32 * q + 32], jnp.where(lane < 96, shifted(0, 64), shifted(1, 96))))
-            far.append(jnp.where(lane < 32, shifted(2, 0), shifted(3, 32)))
-        far = jnp.concatenate(far, axis=0).T
-        inner[pl.ds(i, 128, stride=LAT), :] = jnp.concatenate(near, axis=0).T * (unit[0] * (1.0 / 0.9999))
-        outer[pl.ds(i, 32, stride=LAT), :] = far[:32] * (unit[1] * keep_low)
-        outer[pl.ds(32 * LAT + i, 32, stride=LAT), :] = far[32:64] * (unit[2] * keep_high)
+            edges[0, at:at + LAT, :] = take(edge_ref[0, s, 1 + 3 * k:4 + 3 * k])
+            edges[1, at:at + LAT, :] = take(edge_ref[1, s, 3 * k:3 * k + 3])
+        scales[0, 8 * s:8 * s + 8, :] = value(edge_ref[0, s, 0])
+        scales[1, 8 * s:8 * s + 8, :] = value(edge_ref[1, s, SCALE])
+    for e in range(2):
+        turn_scales(scales.at[e], turned.at[e])
+    place = place_of_latitudes()
+    turn_edges = turner(4)
 
     @pl.loop(0, LAT // GROUP)
     def _(n):
-        for i in range(GROUP):
-            one(n * GROUP + i)
+        for j in range(GROUP):
+            i = n * GROUP + j
+            at, row = place(i)
+            below = jnp.exp(LN2 * turned[0, pl.ds(row, 1), :]) * keep_low
+            above = jnp.exp(LN2 * turned[1, pl.ds(row, 1), :]) * keep_high
+            ends = turn_edges([edges[e, pl.ds(at, 32, stride=LAT), :] for e in range(2)])
+            outer[pl.ds(i, 32, stride=LAT), :] = ends[:, :128] * below
+            outer[pl.ds(32 * LAT + i, 32, stride=LAT), :] = ends[:, 128:] * above
+
+    for copy in loads[1:]:
+        copy.wait()
 
     def level(eo, c, p, r):
         tail = 2 * p + c
@@ -368,6 +421,10 @@
         else:
             ref, at = outer, 32 + eo * 16 + (r - 8) * 8
         return ref[pl.ds(pl.multiple_of((at + tail) * LAT, 8), LAT), :]
+
+    def out_copy(p, side):
+        columns = pl.ds(side * HALF, HALF)
+        return pltpu.make_async_copy(result.at[p, :, :, :, columns], out_ref.at[p, :, :, :, columns], sem.at[p, side])
 
     def potential(p):
         totals = []
@@ -385,27 +442,25 @@
                 result[p, 0, r, :, columns] = level_of[2].astype(BF16)
                 slope = (level_of[0] - level_of[4]) * (1.0 / 12.0) + (level_of[3] - level_of[1]) * (8.0 / 12.0)
                 result[p, 1, r, :, columns] = slope.astype(BF16)
-        pltpu.make_async_copy(result.at[p], out_ref.at[p], sem.at[p]).start()
-
-    if LOOP:
-        @pl.loop(0, POT)
-        def _(p):
-            potential(p)
-    else:
-        for p in range(POT):
-            potential(p)
+            out_copy(p, side).start()
+
+    @pl.loop(0, POT)
+    def _(p):
+        potential(p)
+
     for p in range(POT):
-        pltpu.make_async_copy(result.at[p], out_ref.at[p], sem.at[p]).wait()
+        for side in range(2):
+            out_copy(p, side).wait()
 
 
 def body(coefficients, order_of_slot):
     vmem = pl.BlockSpec(memory_space=pltpu.VMEM)
     anywhere = pl.BlockSpec(memory_space=pl.ANY)
     peers = len(OFFSETS)
-    got, edge, main, tail = pl.pallas_call(
+    inner, edge, main, tail = pl.pallas_call(
         exchange_kernel,
         out_shape=[
-            jax.ShapeDtypeStruct((ORD, UNITS, 8, 128), jnp.int16),
+            jax.ShapeDtypeStruct((128 * LAT, 128), F32),
             jax.ShapeDtypeStruct((2, ORD, EDGE, 8, 128), jnp.int16),
             jax.ShapeDtypeStruct((2, 3 * LDEG, 256), BF16),
             jax.ShapeDtypeStruct((2, 2 * LDEG, 256), BF16),
@@ -420,6 +475,12 @@
             pltpu.VMEM((3, PAIRS, STEP + LDEG, 128), BF16),
             pltpu.VMEM((3, PAIRS, STEP + LDEG, 128), BF16),
             pltpu.VMEM((3, SLOTS * 64, 128), F32),
+            pltpu.VMEM((ORD, UNITS, 8, 128), jnp.int16),
+            pltpu.VMEM((64 * LAT, 128), F32),
+            pltpu.VMEM((2, 32 * LAT, 128), F32),
+            pltpu.VMEM((128, 128), F32),
+            pltpu.VMEM((NLAT, 128), F32),
+            pltpu.VMEM((128 * LAT, 128), F32),
             pltpu.SemaphoreType.DMA((POT * LEV,)),
             pltpu.SemaphoreType.DMA,
             pltpu.SemaphoreType.DMA((peers,)),
@@ -434,19 +495,22 @@
     return pl.pallas_call(
         fourier_kernel,
         out_shape=jax.ShapeDtypeStruct((POT, 2, LEV, LAT, NLON), BF16),
-        in_specs=[vmem] * 4,
+        in_specs=[anywhere] * 4,
         out_specs=anywhere,
         scratch_shapes=[
-            pltpu.VMEM((64 * LAT, 128), F32),
-            pltpu.VMEM((4, 32 * LAT, 128), F32),
-            pltpu.VMEM((3, 128, 128), F32),
-            pltpu.VMEM((3, NLAT, 128), F32),
             pltpu.VMEM((128 * LAT, 128), F32),
+            pltpu.VMEM((2, ORD, EDGE, 8, 128), jnp.int16),
+            pltpu.VMEM((2, 3 * LDEG, 256), BF16),
+            pltpu.VMEM((2, 2 * LDEG, 256), BF16),
+            pltpu.VMEM((2, 32 * LAT, 128), F32),
+            pltpu.VMEM((2, 128, 128), F32),
+            pltpu.VMEM((2, NLAT, 128), F32),
             pltpu.VMEM((64 * LAT, 128), F32),
             pltpu.VMEM((POT, 2, LEV, LAT, NLON), BF16),
-            pltpu.SemaphoreType.DMA((POT,)),
+            pltpu.SemaphoreType.DMA((4,)),
+            pltpu.SemaphoreType.DMA((POT, 2)),
         ],
-    )(got, edge, main, tail)
+    )(inner, edge, main, tail)
 
 
 def solution(mesh):

time: 40.3 us -> 37.7 us (0.935)
  Pallas kernels: 40 us -> 37.5 us
    pallas_call x1, Pallas kernels: 8.21 us -> 6.05 us  [body(): pl.pallas_call(fourier_kernel, out_shape=jax.ShapeDtypeStruct((POT, 2, LE...]
    pallas_call x1, Pallas kernels: 31.8 us -> 31.4 us  [body(): pl.pallas_call(exchange_kernel, out_shape=[jax.ShapeDtypeStruct((128 * LA...]
where the time goes in v4:
time: 37.7 us; the launch traced here: 37.5 us
  Pallas kernels  37.5 us (99%)
    pallas_call x1, Pallas kernels, body(): pl.pallas_call(exchange_kernel, out_shape=[jax.ShapeDtypeStruct((128 * LA...  31.4 us
    pallas_call x1, Pallas kernels, body(): pl.pallas_call(fourier_kernel, out_shape=jax.ShapeDtypeStruct((POT, 2, LE...  6.05 us

profile of v4, /device:TPU:6, one launch (start us, length us, event | category | flops | bytes accessed | tf_op | source)
XLA Modules:
  0.0 37.5 jit_solution(15772454421683145309)
XLA Ops:
  0.0 31.4 %shard_map.28 = (f32[3072,128]{1,0:T(8,128)}, s16[2,16,7,8,128]{4,3,2,1,0:T(8,128)(2,1)}, bf16[2,768,256]{2,1,0:T(8,128)(2,1)}, bf16[2,512,256]{2,1,0:T(8,128)(2,1)}) custom-call(s32[256]{0:T(256)} %order_ref.1, s32[1,256]{1,0:T(1,128)} %bitcast.1, bf16[4,8,16,2,256]{4,3,2,1,0:T(2,128)(2,1)} %coefficients_ref.1), custom_call_target="tpu_custom_call" | custom-call | tf_op jit(solution)/shard_map/pallas_call | solution.py:460
  31.4 6.0 %shard_map.29 = bf16[4,2,8,24,768]{4,3,2,1,0:T(8,128)(2,1)} custom-call(f32[3072,128]{1,0:T(8,128)} %get-tuple-element.9.inner_hbm, s16[2,16,7,8,128]{4,3,2,1,0:T(8,128)(2,1)} %get-tuple-element.10.edge_hbm, bf16[2,768,256]{2,1,0:T(8,128)(2,1)} %get-tuple-element.11.main_hbm, bf16[2,512,256]{2,1,0:T(8,128)(2,1)} %get-tuple-element.12.tail_hbm), custom_call_target="tpu_custom_call" | custom-call | tf_op jit(solution)/shard_map/pallas_call | solution.py:495

commit v5 on v4

--- a/solution.py
+++ b/solution.py
@@ -275,9 +275,9 @@
 
 
 def exchange_kernel(
-    order_ref, heads_ref, coefficients_ref, inner_ref, edge_ref, main_ref, tail_ref,
-    own_ref, coded_ref, fresh, spare, high_table, low_table, sums, got_ref, middle, edges, scales, turned, inner,
-    load_sem, out_sem, send_sem, recv_sem, up_send, up_recv, down_send, down_recv,
+    order_ref, heads_ref, coefficients_ref, inner_ref, edge_ref, main_out, tail_out,
+    main_ref, tail_ref, own_ref, coded_ref, fresh, spare, high_table, low_table, sums, got_ref, middle, edges, scales, turned, inner,
+    load_sem, out_sem, wave_sem, send_sem, recv_sem, up_send, up_recv, down_send, down_recv,
 ):
     me = lax.axis_index("ord")
     y, x = me // SIDE, me % SIDE
@@ -339,8 +339,14 @@
 
     pass_on(coded_ref.at[me], me, len(OFFSETS))
     wave_tables(heads_ref, main_ref, tail_ref)
+    waves = [
+        pltpu.make_async_copy(main_ref, main_out, wave_sem.at[0]),
+        pltpu.make_async_copy(tail_ref, tail_out, wave_sem.at[1]),
+    ]
+    for copy in waves:
+        copy.start()
     unpack(coded_ref, me)
-    for n, (dy, dx) in enumerate(OFFSETS):
+    for n, (dy, dx) in reversed(list(enumerate(OFFSETS))):
         sends[n].wait_recv()
         source = other(SIDE - dy, SIDE - dx)
         pass_on(got_ref.at[source], source, n)
@@ -366,6 +372,8 @@
     for copy in sends:
         copy.wait_send()
     for copy in passed:
+        copy.wait()
+    for copy in waves:
         copy.wait()
     result.wait()
 
@@ -466,8 +474,10 @@
             jax.ShapeDtypeStruct((2, 2 * LDEG, 256), BF16),
         ],
         in_specs=[pl.BlockSpec(memory_space=pltpu.SMEM), vmem, anywhere],
-        out_specs=[anywhere, anywhere, vmem, vmem],
+        out_specs=[anywhere] * 4,
         scratch_shapes=[
+            pltpu.VMEM((2, 3 * LDEG, 256), BF16),
+            pltpu.VMEM((2, 2 * LDEG, 256), BF16),
             pltpu.VMEM((SLOTS, LEV, POT, 2, LDEG), BF16),
             pltpu.VMEM((ORD, UNITS, 8, 128), jnp.int16),
             pltpu.VMEM((3, PAIRS * STEP, 128), F32),
@@ -483,6 +493,7 @@
             pltpu.VMEM((128 * LAT, 128), F32),
             pltpu.SemaphoreType.DMA((POT * LEV,)),
             pltpu.SemaphoreType.DMA,
+            pltpu.SemaphoreType.DMA((2,)),
             pltpu.SemaphoreType.DMA((peers,)),
             pltpu.SemaphoreType.DMA((peers,)),
             pltpu.SemaphoreType.DMA((ORD,)),

time: 37.7 us -> 38.4 us (1.019)
  Pallas kernels: 37.5 us -> 38.3 us
    pallas_call x1, Pallas kernels: 31.4 us -> 32.2 us  [body(): pl.pallas_call(exchange_kernel, out_shape=[jax.ShapeDtypeStruct((128 * LA...]
where the time goes in v5:
time: 38.4 us; the launch traced here: 38.3 us
  Pallas kernels  38.3 us (100%)
    pallas_call x1, Pallas kernels, body(): pl.pallas_call(exchange_kernel, out_shape=[jax.ShapeDtypeStruct((128 * LA...  32.2 us
    pallas_call x1, Pallas kernels, body(): pl.pallas_call(fourier_kernel, out_shape=jax.ShapeDtypeStruct((POT, 2, LE...  6.05 us

profile of v5, /device:TPU:6, one launch (start us, length us, event | category | flops | bytes accessed | tf_op | source)
XLA Modules:
  0.0 38.3 jit_solution(14041389131951200198)
XLA Ops:
  0.0 32.2 %shard_map.28 = (f32[3072,128]{1,0:T(8,128)}, s16[2,16,7,8,128]{4,3,2,1,0:T(8,128)(2,1)}, bf16[2,768,256]{2,1,0:T(8,128)(2,1)}, bf16[2,512,256]{2,1,0:T(8,128)(2,1)}) custom-call(s32[256]{0:T(256)} %order_ref.1, s32[1,256]{1,0:T(1,128)} %bitcast.1, bf16[4,8,16,2,256]{4,3,2,1,0:T(2,128)(2,1)} %coefficients_ref.1), custom_call_target="tpu_custom_call" | custom-call | tf_op jit(solution)/shard_map/pallas_call | solution.py:468
  32.2 6.0 %shard_map.29 = bf16[4,2,8,24,768]{4,3,2,1,0:T(8,128)(2,1)} custom-call(f32[3072,128]{1,0:T(8,128)} %get-tuple-element.9.inner_hbm, s16[2,16,7,8,128]{4,3,2,1,0:T(8,128)(2,1)} %get-tuple-element.10.edge_hbm, bf16[2,768,256]{2,1,0:T(8,128)(2,1)} %get-tuple-element.11.main_hbm, bf16[2,512,256]{2,1,0:T(8,128)(2,1)} %get-tuple-element.12.tail_hbm), custom_call_target="tpu_custom_call" | custom-call | tf_op jit(solution)/shard_map/pallas_call | solution.py:506
